TPU v7x, 256 devices: a whole 4x4x8 slice. The times are simulated.
256 devices in a mesh: ctx: 32 (over y_lo, z, core), tp: 8 (over y_hi, x).
Axes of the slice: x: 4, y: 4 (y_hi: 2, y_lo: 2; y = y_hi * 2 + y_lo), z: 8, core: 2. Of those that a mesh axis runs over, the one named last changes fastest.
Arguments:
- tokens_clean: bfloat16 [4096, 4096], P(('ctx', 'tp')), may hold values from -6 to 6
- noise_mask: int32 [4096], P(('ctx', 'tp')), may hold values 0 or 1
- mask_embed: bfloat16 [4096], replicated, may hold values from -6 to 6
- norm_gain: bfloat16 [4096], replicated, may hold values from 0.099609375 to 1.8984375
- w_query: bfloat16 [4096, 2048], P(None, 'tp'), may hold values from -0.375 to 0.375
- w_key: bfloat16 [4096, 2048], P(None, 'tp'), may hold values from -0.375 to 0.375
- w_value: bfloat16 [4096, 2048], P(None, 'tp'), may hold values from -0.09375 to 0.09375
- w_out: bfloat16 [2048, 4096], P('tp'), may hold values from -0.5 to 0.5
- block_mask: int32 [128, 128], replicated, may hold values from 0 to 3, as said below
Outputs:
- clean_out: bfloat16 [4096, 4096], P(('ctx', 'tp'))
- noisy_out: bfloat16 [4096, 4096], P(('ctx', 'tp'))
Inputs may be any that keep to these rules, and one draw needn't show every extreme that they name: `block_mask`: entry (i, j) is a + 2 b: a = 1 where clean block i sees clean block j, b = 1 where noisy block i sees clean block j. For each i the j with a = 1 form one run ending at j = i, and those with b = 1 one run ending at j = i - 1, or none; entries with j > i are 0.
All inputs are finite; a program needn't handle non-finite values. No bound on the sum of `noise_mask` on one device may be relied on, other than what follows from the above.
Results may differ from a plain program's by a relative error of at most 0.014.
Values may be sent and summed in bfloat16 or wider, within the bound.
No kernel may reach another device: no remote copies, remote signals or barrier semaphores. Data moves between devices by JAX's collectives and lax.ppermute only.
A program may use at most 128 MiB of HBM per device.

v0:
```python
import jax
import jax.numpy as jnp
from jax import lax
from jax.sharding import PartitionSpec as P

HEAD_DIM = 128
BLOCK = 32


ROPE_BASE = 500000.0
EPSILON = 1e-05
NEG_FILL = -1e30


def rms_rows(values, gain):
    wide = values.astype(jnp.float32)
    factor = lax.rsqrt(jnp.mean(wide * wide, axis=-1, keepdims=True) + EPSILON)
    return (wide * factor * gain.astype(jnp.float32)).astype(jnp.bfloat16)


def rotate(values, positions):
    half_dim = values.shape[-1] // 2
    indices = jnp.arange(half_dim).astype(jnp.float32)
    freqs = ROPE_BASE ** (-2.0 * indices / values.shape[-1])
    angles = positions.astype(jnp.float32)[:, None] * freqs[None, :]
    cosine = jnp.cos(angles)[:, None, :]
    sine = jnp.sin(angles)[:, None, :]
    lower = values[..., :half_dim]
    upper = values[..., half_dim:]
    return jnp.concatenate([lower * cosine - upper * sine, upper * cosine + lower * sine], axis=-1)


def start_state(heads, length):
    return (
        jnp.full((heads, length), NEG_FILL, jnp.float32),
        jnp.zeros((heads, length), jnp.float32),
        jnp.zeros((heads, length, HEAD_DIM), jnp.float32),
    )


def attend(state, queries, keys, values, visible):
    peak_old, total_old, weighted_old = state
    scores = jnp.einsum(
        "qhd,khd->hqk", queries, keys, preferred_element_type=jnp.float32
    ) * HEAD_DIM ** (-0.5)
    scores = jnp.where(visible[None], scores, NEG_FILL)
    peak_new = jnp.maximum(peak_old, jnp.max(scores, axis=-1))
    weights = jnp.where(visible[None], jnp.exp(scores - peak_new[..., None]), 0.0)
    factor = jnp.exp(peak_old - peak_new)
    total_new = total_old * factor + jnp.sum(weights, axis=-1)
    weighted_new = weighted_old * factor[..., None] + jnp.einsum(
        "hqk,khd->hqd", weights.astype(jnp.bfloat16), values, preferred_element_type=jnp.float32
    )
    return (peak_new, total_new, weighted_new)


def local(
    tokens_clean, noise_mask, mask_embed, norm_gain, w_query, w_key, w_value, w_out, block_mask
):
    normed = rms_rows(tokens_clean, norm_gain)
    mask_row = rms_rows(mask_embed[None, :], norm_gain)
    gathered, noise_flags = (
        lax.all_gather(normed, "tp", axis=0, tiled=True),
        lax.all_gather(noise_mask, "tp", axis=0, tiled=True),
    )
    local_len = gathered.shape[0]
    width = w_query.shape[1]
    heads = width // HEAD_DIM
    first_row = lax.axis_index("ctx") * local_len
    positions = first_row + jnp.arange(local_len, dtype=jnp.int32)
    noisy_rows = (noise_flags == 1)[:, None]

    def project(weight, rotary):
        clean = jnp.dot(gathered, weight, preferred_element_type=jnp.float32)
        masked = jnp.dot(mask_row, weight, preferred_element_type=jnp.float32)
        noisy = jnp.where(noisy_rows, masked, clean)
        clean = clean.reshape(local_len, heads, HEAD_DIM)
        noisy = noisy.reshape(local_len, heads, HEAD_DIM)
        if rotary:
            clean = rotate(clean, positions)
            noisy = rotate(noisy, positions)
        return (clean.astype(jnp.bfloat16), noisy.astype(jnp.bfloat16))

    q_clean, q_noisy = project(w_query, True)
    k_clean, k_noisy = project(w_key, True)
    v_clean, v_noisy = project(w_value, False)
    key_values = jnp.stack([k_clean.reshape(local_len, width), v_clean.reshape(local_len, width)])

    def finish(state):
        weighted = state[2] / state[1][..., None]
        return jnp.transpose(weighted, (1, 0, 2)).reshape(local_len, width).astype(jnp.bfloat16)

    row_table = jnp.take(block_mask, positions // BLOCK, axis=0)
    own_block = (positions // BLOCK)[:, None] == (positions // BLOCK)[None, :]
    noisy_state = attend(start_state(heads, local_len), q_noisy, k_noisy, v_noisy, own_block)
    states = (start_state(heads, local_len), noisy_state)
    piece = lax.all_gather(key_values, "ctx", axis=1, tiled=True)
    count = piece.shape[1]
    visible = jnp.repeat(row_table, BLOCK, axis=1)
    keys = piece[0].reshape(count, heads, HEAD_DIM)
    values = piece[1].reshape(count, heads, HEAD_DIM)
    states = (
        attend(states[0], q_clean, keys, values, visible % 2 == 1),
        attend(states[1], q_noisy, keys, values, visible // 2 == 1),
    )
    attended = jnp.stack([finish(states[0]), finish(states[1])])
    model_width = w_out.shape[1]
    piece = attended
    summed = lax.psum_scatter(
        jnp.einsum("sqc,cd->qsd", piece, w_out, preferred_element_type=jnp.float32)
        .reshape(local_len // lax.axis_size("tp") * lax.axis_size("tp"), 2 * model_width)
        .astype(jnp.bfloat16),
        "tp",
        scatter_dimension=0,
        tiled=True,
    ).astype(jnp.float32)
    result = summed.reshape(summed.shape[0], 2, model_width)
    return (result[:, 0].astype(jnp.bfloat16), result[:, 1].astype(jnp.bfloat16))


def solution(mesh):
    return jax.shard_map(
        local,
        mesh=mesh,
        in_specs=(
            P(("ctx", "tp"), None),
            P(("ctx", "tp")),
            P(),
            P(),
            P(None, "tp"),
            P(None, "tp"),
            P(None, "tp"),
            P("tp", None),
            P(),
        ),
        out_specs=(P(("ctx", "tp"), None), P(("ctx", "tp"), None)),
        check_vma=False,
    )
```

profile of v0, /device:TPU:32, one launch (start us, length us, event | category | flops | bytes accessed | tf_op | source)
XLA Modules:
  0.0 276.8 jit_solution(12678092946589424818)
XLA Ops:
  7.2 1.2 fusion.52
  9.1 1.7 fusion.54
  10.9 1.3 fusion.70
  13.6 1.3 dynamic-slice
  16.4 13.7 %all-reduce = s32[128]{0:T(128)S(1)} all-reduce(s32[128]{0:T(128)S(1)} %dynamic-update-slice), channel_id=1, replica_groups=mesh['ctx'=32,'tp'=8] {'tp'}, use_global_device_ids=true, to_apply=%add | all-reduce | flops 128 | bytes 1024
  31.6 2.1 fusion.100
  34.5 31.5 %all-gather.3.cloned.1.call-done = bf16[128,4096]{1,0:T(8,128)(2,1)} async-done(((bf16[16,4096]{1,0:T(8,128)(2,1)}), bf16[128,4096]{1,0:T(8,128)(2,1)}) %all-gather.3.cloned.1.call-update) | async-done | bytes 1048592 | tf_op jit(solution)/shard_map/all_gather | solution.py:63
  66.1 2.4 fusion.97
  68.6 2.7 broadcast_select_fusion
  72.3 1.6 reshape.370
  74.0 1.3 fusion.92
  76.7 2.0 select_convert_fusion
  80.6 1.5 fusion.9
  82.9 1.8 copy.87
  87.0 57.1 %all-gather.5.cloned.1.call-done = bf16[2,4096,256]{2,1,0:T(8,128)(2,1)} async-done(((bf16[2,128,256]{2,1,0:T(8,128)(2,1)}), bf16[2,4096,256]{2,1,0:T(8,128)(2,1)}) %all-gather.5.cloned.1.call-update) | async-done | bytes 4194320 | tf_op jit(solution)/shard_map/all_gather | solution.py:97
  144.2 4.5 %fusion.88 = (bf16[1,4096,256]{2,1,0:T(8,128)(2,1)}, bf16[1,4096,256]{2,1,0:T(8,128)(2,1)}) fusion(bf16[2,4096,256]{2,1,0:T(8,128)(2,1)} %all-gather.5.cloned.1.call-done), kind=kLoop, calls=%fused_computation.136 | loop fusion | bytes 8388608 | tf_op jit(solution)/shard_map/slice | solution.py:100
  148.7 4.0 %reshape_squeeze.6 = bf16[4096,2,128]{2,1,0:T(2,128)(2,1)} reshape(bf16[1,4096,256]{2,1,0:T(8,128)(2,1)} %get-tuple-element.4) | data formatting | bytes 4194304 | tf_op jit(solution)/shard_map/reshape;squeeze | solution.py:100
  152.6 4.1 %copy.99 = bf16[1,4096,256]{1,2,0:T(8,128)(2,1)} copy(bf16[1,4096,256]{2,1,0:T(8,128)(2,1)} %get-tuple-element.5) | data formatting | bytes 4194304 | tf_op jit(solution)/shard_map/reshape;squeeze | solution.py:101
  156.8 3.0 %fusion.95 = (f32[2,128]{1,0:T(2,128)S(1)}, f32[2,128,4096]{2,1,0:T(8,128)S(1)}) fusion(bf16[4096,2,128]{2,1,0:T(2,128)(2,1)} %reshape_squeeze.6, bf16[128,2,64]{2,0,1:T(8,128)(2,1)S(1)} %get-tuple-element.18, bf16[128,2,64]{2,0,1:T(8,128)(2,1)S(1)} %get-tuple-element.19, pred[128,4096]{1,0:T(8,128)(4,1)S(1)} %copy.87), kind=kOutput, calls=%fused_computation.143 | convolution fusion | flops 271712000 | bytes 6882304 | tf_op jit(solution)/shard_map/qhd,khd->hqk/dot_general | solution.py:43
  159.8 1.1 fusion.5
  161.4 1.0 fusion.39
  162.8 3.0 %fusion.96 = (f32[2,128]{1,0:T(2,128)S(1)}, f32[2,128,4096]{2,1,0:T(8,128)S(1)}) fusion(bf16[4096,2,128]{2,1,0:T(2,128)(2,1)} %reshape_squeeze.6, bf16[128,2,64]{2,0,1:T(8,128)(2,1)S(1)} %copy-done.12, bf16[128,2,64]{2,0,1:T(8,128)(2,1)S(1)} %copy-done.11, pred[128,4096]{1,0:T(8,128)(4,1)S(1)} %copy.73), kind=kOutput, calls=%fused_computation.144 | convolution fusion | flops 271712000 | bytes 6882304 | tf_op jit(solution)/shard_map/qhd,khd->hqk/dot_general | solution.py:43
  165.8 1.1 fusion.3
  167.4 1.4 fusion.49
  168.9 2.0 fusion.2
  170.9 4.1 %copy.92 = bf16[128,2,4096]{0,2,1:T(8,128)(2,1)} copy(bf16[128,2,4096]{2,0,1:T(8,128)(2,1)} %fusion.2) | data formatting | bytes 4194304 | tf_op jit(solution)/shard_map/convert_element_type | solution.py:112
  175.0 4.1 %copy.97 = bf16[128,8192]{1,0:T(8,128)(2,1)} copy(bf16[128,8192]{0,1:T(8,128)(2,1)} %bitcast.133) | data formatting | bytes 4194304
  179.1 82.7 %reduce-scatter.4.cloned.1.call-done = bf16[16,8192]{1,0:T(8,128)(2,1)} async-done(((bf16[128,8192]{1,0:T(8,128)(2,1)}), bf16[16,8192]{1,0:T(8,128)(2,1)}) %reduce-scatter.4.cloned.1.call-update) | async-done | bytes 262160
  261.8 2.6 copy.98
  264.5 2.7 fusion.89
  267.1 2.2 copy.101
  269.3 1.0 copy.100
  (73 shorter events, 13.7 us)
Async XLA Ops:
  7.2 161.7 %copy-start = (bf16[256,4096]{1,0:T(8,128)(2,1)S(1)}, bf16[256,4096]{1,0:T(8,128)(2,1)}, u32[]{:S(2)}) copy-start(bf16[256,4096]{1,0:T(8,128)(2,1)} %param.16) | copy-start | bytes 6291460
  7.2 58.9 %all-gather.3.cloned.1.call-start = ((), (), s32[]{:S(2)}) async-start(), calls=%async_computation.1 | async-start | bytes 1179648 | tf_op jit(solution)/shard_map/all_gather | solution.py:63
  10.8 133.4 %all-gather.5.cloned.1.call-start = ((), (), s32[]{:S(2)}) async-start(), calls=%async_computation.2 | async-start | bytes 4325376 | tf_op jit(solution)/shard_map/all_gather | solution.py:97
  30.1 3.7 %copy-start.2 = (bf16[4096,256]{1,0:T(8,128)(2,1)S(1)}, bf16[4096,256]{1,0:T(8,128)(2,1)}, u32[]{:S(2)}) copy-start(bf16[4096,256]{1,0:T(8,128)(2,1)} %param.14) | copy-start | bytes 6291460
  31.6 2.5 copy-start.3
  66.1 2.5 copy-start.1
  74.0 1.7 copy-start.8
  74.0 1.7 copy-start.9
  76.5 3.2 %copy-start.4 = (s32[128,128]{1,0:T(8,128)S(1)}, s32[128,128]{1,0:T(8,128)}, u32[]{:S(2)}) copy-start(s32[128,128]{1,0:T(8,128)} %param.17) | copy-start | bytes 196612
  79.5 182.4 %reduce-scatter.4.cloned.1.call-start = ((), (), s32[]{:S(2)}) async-start(), calls=%async_computation.3 | async-start | bytes 2359296
  79.7 6.5 %copy-start.7 = (bf16[128,2,64]{2,0,1:T(8,128)(2,1)S(1)}, bf16[128,2,64]{2,0,1:T(8,128)(2,1)}, u32[]{:S(2)}) copy-start(bf16[128,2,64]{2,0,1:T(8,128)(2,1)} %get-tuple-element.21) | copy-start | bytes 98308
  156.7 3.0 %copy-start.13 = (f32[2,128]{1,0:T(2,128)S(1)}, f32[2,128]{1,0:T(2,128)}, u32[]{:S(2)}) copy-start(f32[2,128]{1,0:T(2,128)} %get-tuple-element.42) | copy-start | bytes 3076
  159.8 1.6 copy-start.5
  161.4 1.1 copy-start.10
  161.4 1.4 copy-start.11
  161.4 1.4 copy-start.12
  165.8 1.6 copy-start.6
Sparse Core Ops, SparseCore 0:
  11.2 54.8 all-gather.2
  79.6 64.5 all-gather.4
  179.3 82.5 reduce-scatter.3
where the time goes:
time: 278 us; the launch traced here: 277 us
  waiting for transfers between devices  171 us (62%)
  local copies, waits for them, and re-layouts  41.2 us (15%)
  matrix products  21.5 us (8%)
  between operations  15.4 us (6%)
  blocking collectives  13.7 us (5%)
  other arithmetic  13.3 us (5%)
    unnamed x4, waiting for transfers between devices  82.7 us
    all_gather x1, waiting for transfers between devices, local(): piece = lax.all_gather(key_values, 'ctx', axis=1, tiled=True)  57.1 us
    all_gather x1, waiting for transfers between devices, local(): lax.all_gather(normed, 'tp', axis=0, tiled=True)  31.5 us
    unnamed x1, blocking collectives  13.7 us
    unnamed x34, local copies, waits for them, and re-layouts  13.1 us
    dot_general x3, matrix products, project(): clean = jnp.dot(gathered, weight, preferred_element_type=jnp.float32)  7.17 us
    dot_general x3, matrix products, attend(): jnp.einsum('qhd,khd->hqk', queries, keys, preferred_element_type=jnp.floa...  6.77 us
  transfers between devices with their start and end apart: 3, of which 3 were waited for; matrix products, arithmetic and copies ran while one was open for 6% of the time, Pallas kernels for 0%

commit v1 on v0

v1 whole, which is shorter than its diff:
```python
import jax
import jax.numpy as jnp
from jax import lax
from jax.experimental import pallas as pl
from jax.experimental.pallas import tpu as pltpu
from jax.sharding import PartitionSpec as P


HEAD_DIM = 128
BLOCK = 32
ROPE_BASE = 500000.0
EPSILON = 1e-05
TOK = 128
D = 4096
NZ = 8
NT = 8
LOG2E = 1.4426950408889634
SCALE2 = HEAD_DIM ** (-0.5) * LOG2E
HIDDEN = -1e30
FLOOR = -1e29
TERMS_PP = False


VMEM = pl.BlockSpec(memory_space=pltpu.VMEM)
ANY = pl.BlockSpec(memory_space=pl.ANY)
HBM = pl.BlockSpec(memory_space=pltpu.HBM)
SMEM = pl.BlockSpec(memory_space=pltpu.SMEM)


def params(mib=16):
    return pltpu.CompilerParams(vmem_limit_bytes=mib << 20)


def cost(mib, flops=1 << 20):
    return pl.CostEstimate(flops=flops, bytes_accessed=mib << 20, transcendentals=0)


def struct(*shape, dtype=jnp.bfloat16):
    return jax.ShapeDtypeStruct(shape, dtype)


def head(h):
    return slice(h * HEAD_DIM, (h + 1) * HEAD_DIM)


def relative(me, r):
    return ((me // 4) ^ (r // 4)) * 4 + (me + r) % 4


def norm_kernel(tok_hbm, flag_hbm, mask_hbm, gain_hbm, out_ref, mask_out_ref, tok, flag, mask, gain, sems):
    copies = [
        pltpu.make_async_copy(src, dst, sems.at[i])
        for i, (src, dst) in enumerate(
            ((tok_hbm, tok), (flag_hbm, flag), (mask_hbm, mask), (gain_hbm, gain))
        )
    ]
    for copy in copies:
        copy.start()
    for copy in copies:
        copy.wait()
    wide_gain = gain[...].astype(jnp.float32)
    row = lax.broadcasted_iota(jnp.int32, (16, 128), 0)
    flags = jnp.zeros((16, 128), jnp.float32)
    for i in range(16):
        flags = jnp.where(row == i, flag[i].astype(jnp.float32), flags)
    out_ref[:, D:] = flags.astype(jnp.bfloat16)
    wide = tok[...].astype(jnp.float32)
    factor = lax.rsqrt(jnp.mean(wide * wide, axis=-1, keepdims=True) + EPSILON)
    wide_mask = mask[...].astype(jnp.float32)
    square = jnp.sum(wide_mask * wide_mask, axis=0, keepdims=True)
    factor_mask = lax.rsqrt(jnp.sum(square, axis=1, keepdims=True) / D + EPSILON)
    mask_row = wide_mask * factor_mask * wide_gain
    for j in range(D // 128):
        lanes = slice(j * 128, (j + 1) * 128)
        out_ref[:, lanes] = (wide[:, lanes] * factor * wide_gain[j : j + 1]).astype(jnp.bfloat16)
        mask_out_ref[:, lanes] = jnp.broadcast_to(mask_row[j : j + 1], (16, 128)).astype(jnp.bfloat16)


def norm(tokens, flags, mask_embed, gain):
    return pl.pallas_call(
        norm_kernel,
        out_shape=(struct(16, D + 128), struct(16, D)),
        in_specs=[HBM] * 4,
        out_specs=(VMEM, VMEM),
        scratch_shapes=[
            pltpu.VMEM((16, D), jnp.bfloat16),
            pltpu.SMEM((16,), jnp.int32),
            pltpu.VMEM((D // 128, 128), jnp.bfloat16),
            pltpu.VMEM((D // 128, 128), jnp.bfloat16),
            pltpu.SemaphoreType.DMA((4,)),
        ],
        compiler_params=params(),
        cost_estimate=cost(1),
        name="norm",
    )(tokens, flags, mask_embed.reshape(D // 128, 128), gain.reshape(D // 128, 128))


def weights_kernel(mask_ref, wq_hbm, wk_hbm, wv_hbm, w_ref, masked_ref, sems):
    parts = 4
    depth = D // parts
    copies = []
    for i, src in enumerate((wk_hbm, wv_hbm, wq_hbm)):
        for p in range(parts):
            rows = pl.ds(p * depth, depth)
            copies.append(
                pltpu.make_async_copy(src.at[rows, :], w_ref.at[rows, pl.ds(i * 256, 256)], sems.at[i, p])
            )
    for copy in copies:
        copy.start()
    for copy in copies:
        copy.wait()
    for i in range(3):
        masked_ref[:, i * 256 : (i + 1) * 256] = jnp.dot(
            mask_ref[...], w_ref[:, i * 256 : (i + 1) * 256], preferred_element_type=jnp.float32
        )[:8]


def load_weights(mask_row, wq, wk, wv):
    return pl.pallas_call(
        weights_kernel,
        out_shape=(struct(D, 768), struct(8, 768, dtype=jnp.float32)),
        in_specs=[VMEM, HBM, HBM, HBM],
        out_specs=(VMEM, VMEM),
        scratch_shapes=[pltpu.SemaphoreType.DMA((3, 4))],
        compiler_params=params(),
        cost_estimate=cost(12),
        name="weights",
    )(mask_row, wq, wk, wv)


def place():
    ctx = lax.axis_index("ctx")
    return ctx // 16, (ctx // 2) % NZ, ctx % 2


def rotary(v, cosine, sine):
    return v * cosine + pltpu.roll(v, HEAD_DIM // 2, 1) * sine


def both(rows_ref, w_ref, masked_ref, i):
    cols = slice(i * 256, (i + 1) * 256)
    noisy = rows_ref[:, D : D + 1].astype(jnp.float32) > 0.5
    clean = jnp.dot(rows_ref[:, :D], w_ref[:, cols], preferred_element_type=jnp.float32)
    return clean, jnp.where(noisy, masked_ref[0:1, cols], clean)


def key_kernel(*refs):
    g_refs = refs[:NT]
    w_ref, masked_ref, cos_ref, sin_ref, kv_ref, kvn_ref, rows_ref = refs[NT:]
    me = lax.axis_index("tp")
    for r in range(NT):
        rows_ref[pl.ds(pl.multiple_of(relative(me, r) * 16, 16), 16), :] = g_refs[r][...]
    cosine, sine = cos_ref[...], sin_ref[...]
    keys = both(rows_ref, w_ref, masked_ref, 0)
    values = both(rows_ref, w_ref, masked_ref, 1)
    for h in range(2):
        for k, v, ref in zip(keys, values, (kv_ref, kvn_ref)):
            ref[:, head(h)] = rotary(k[:, head(h)], cosine, sine).astype(jnp.bfloat16)
            ref[:, head(2 + h)] = v[:, head(h)].astype(jnp.bfloat16)


def project_keys(gathered, w, masked, cosine, sine):
    return pl.pallas_call(
        key_kernel,
        out_shape=(struct(TOK, 512), struct(TOK, 512), struct(TOK, D + 128)),
        in_specs=[VMEM] * (NT + 4),
        out_specs=(VMEM,) * 3,
        compiler_params=params(),
        cost_estimate=cost(6, 1 << 30),
        name="keys",
    )(*gathered, w, masked, cosine, sine)


def query_kernel(rows_ref, w_ref, masked_ref, cos_ref, sin_ref, q_ref):
    cosine, sine = cos_ref[...], sin_ref[...]
    for i, q in enumerate(both(rows_ref, w_ref, masked_ref, 2)):
        for h in range(2):
            q_ref[i * TOK : (i + 1) * TOK, head(h)] = rotary(q[:, head(h)], cosine, sine).astype(jnp.bfloat16)


def project_queries(rows, w, masked, cosine, sine):
    return pl.pallas_call(
        query_kernel,
        out_shape=struct(2 * TOK, 256),
        in_specs=[VMEM] * 5,
        out_specs=VMEM,
        compiler_params=params(),
        cost_estimate=cost(3, 1 << 29),
        name="queries",
    )(rows, w, masked, cosine, sine)


def pack_stats(lses):
    rows = lses[0].shape[0]
    lane = lax.broadcasted_iota(jnp.int32, (rows, 128), 1)
    total = jnp.zeros((rows, 128), jnp.float32)
    for h, lse in enumerate(lses):
        rest = lse
        for part in range(3):
            piece = rest.astype(jnp.bfloat16).astype(jnp.float32)
            total = jnp.where(lane == h * 4 + part, piece, total)
            rest = rest - piece
    return total.astype(jnp.bfloat16)


def unpack_stats(block):
    wide = block.astype(jnp.float32)
    return [
        wide[:, h * 4 : h * 4 + 1] + wide[:, h * 4 + 1 : h * 4 + 2] + wide[:, h * 4 + 2 : h * 4 + 3]
        for h in range(2)
    ]


def attend_kernel(far, *refs):
    table_ref, mine_ref, other_ref = refs[:3]
    kv_refs = refs[3 : 3 + NZ]
    rest = refs[3 + NZ :]
    kvn_ref = None if far else rest[0]
    out_mine, out_other, keys = rest[-3:]
    y, z, c = place()
    col = lax.broadcasted_iota(jnp.int32, (1, NZ * TOK), 1)

    def work():
        for s in range(NZ):
            keys[s * TOK : (s + 1) * TOK, :] = kv_refs[s][...]
        source = (z - col // TOK) & (NZ - 1)
        key_block = (y * 16 + source * 2 + c) * 4 + (col % TOK) // BLOCK
        part = lax.broadcasted_iota(jnp.int32, (2 * TOK, 1), 0) // BLOCK
        for g, q_ref, out_ref in ((1, other_ref, out_other), (0, mine_ref, out_mine)):
            yq = 1 if far else y
            cq = c if g == 0 else 1 - c
            first = (yq * 16 + z * 2 + cq) * 4
            low = jnp.zeros((2 * TOK, 1), jnp.int32)
            high = jnp.zeros((2 * TOK, 1), jnp.int32)
            for p in range(8):
                copy, block = p // 4, first + p % 4
                low = jnp.where(part == p, table_ref[copy, block], low)
                high = jnp.where(part == p, block - copy, high)
            visible = (key_block >= low) & (key_block <= high)
            lses = []
            for h in range(2):
                q = q_ref[:, head(h)]
                scores = lax.dot_general(
                    q, keys[:, head(h)], (((1,), (1,)), ((), ())), preferred_element_type=jnp.float32
                ) * SCALE2
                scores = jnp.where(visible, scores, HIDDEN)
                peak = jnp.maximum(jnp.max(scores, axis=-1, keepdims=True), FLOOR)
                near_part = g == 0 and not far
                if near_part:
                    own = lax.dot_general(
                        q[TOK:], kvn_ref[:, head(h)], (((1,), (1,)), ((), ())),
                        preferred_element_type=jnp.float32,
                    ) * SCALE2
                    near = (
                        lax.broadcasted_iota(jnp.int32, (TOK, TOK), 0) // BLOCK
                        == lax.broadcasted_iota(jnp.int32, (TOK, TOK), 1) // BLOCK
                    )
                    own = jnp.where(near, own, HIDDEN)
                    peak_own = jnp.maximum(peak[TOK:], jnp.max(own, axis=-1, keepdims=True))
                    peak = jnp.concatenate([peak[:TOK], peak_own], axis=0)
                weights = jnp.exp2(scores - peak)
                total = jnp.sum(weights, axis=-1, keepdims=True)
                weighted = jnp.dot(
                    weights.astype(jnp.bfloat16), keys[:, head(2 + h)], preferred_element_type=jnp.float32
                )
                if near_part:
                    wown = jnp.exp2(own - peak_own)
                    total = total + jnp.concatenate(
                        [jnp.zeros((TOK, 1), jnp.float32), jnp.sum(wown, axis=-1, keepdims=True)], axis=0
                    )
                    extra = jnp.dot(
                        wown.astype(jnp.bfloat16), kvn_ref[:, head(2 + h)], preferred_element_type=jnp.float32
                    )
                    weighted = weighted + jnp.concatenate(
                        [jnp.zeros((TOK, HEAD_DIM), jnp.float32), extra], axis=0
                    )
                some = total > 0.0
                safe = jnp.where(some, total, 1.0)
                out_ref[:, head(h)] = (weighted / safe).astype(jnp.bfloat16)
                lses.append(jnp.where(some, peak + jnp.log2(safe), FLOOR))
            out_ref[:, 256:] = pack_stats(lses)

    if far:
        pl.when(y == 0)(work)

        @pl.when(y == 1)
        def _():
            out_mine[...] = jnp.zeros_like(out_mine)
            out_other[...] = jnp.zeros_like(out_other)
    else:
        work()


def attend(table, mine, other, key_values, *extra):
    far = not extra

    def kernel(*refs):
        attend_kernel(far, *refs)

    return pl.pallas_call(
        kernel,
        out_shape=(struct(2 * TOK, 384), struct(2 * TOK, 384)),
        in_specs=[SMEM] + [VMEM] * (2 + NZ) + ([] if far else [VMEM, ANY]),
        out_specs=(VMEM, VMEM),
        scratch_shapes=[pltpu.VMEM((NZ * TOK, 512), jnp.bfloat16)],
        compiler_params=params(),
        cost_estimate=cost(4, 1 << 29),
        name="attend_far" if far else "attend_near",
    )(table, mine, other, *key_values, *extra)


def merge(a, b):
    outs, lses = [], []
    sa, sb = unpack_stats(a[:, 256:]), unpack_stats(b[:, 256:])
    for h in range(2):
        peak = jnp.maximum(sa[h], sb[h])
        wa, wb = jnp.exp2(sa[h] - peak), jnp.exp2(sb[h] - peak)
        total = wa + wb
        mixed = a[:, head(h)].astype(jnp.float32) * wa + b[:, head(h)].astype(jnp.float32) * wb
        outs.append(mixed / total)
        lses.append(peak + jnp.log2(total))
    return outs, lses


def merge_kernel(mine_ref, swap_ref, out_ref):
    outs, lses = merge(mine_ref[...], swap_ref[...])
    for h in range(2):
        out_ref[:, head(h)] = outs[h].astype(jnp.bfloat16)
    out_ref[:, 256:] = pack_stats(lses)


def merge_cores(mine, swapped):
    return pl.pallas_call(
        merge_kernel,
        out_shape=struct(2 * TOK, 384),
        in_specs=[VMEM, VMEM],
        out_specs=VMEM,
        compiler_params=params(),
        cost_estimate=cost(1),
    )(mine, swapped)


def output_kernel(self_ref, far_ref, w_ref, *refs):
    att = refs[-1]
    outs, _ = merge(self_ref[...], far_ref[...])
    upper_line = place()[0] == 1
    for h in range(2):
        alone = self_ref[:, head(h)].astype(jnp.float32)
        value = jnp.where(upper_line, outs[h], alone).astype(jnp.bfloat16)
        for t in range(NT):
            for s in range(2):
                att[t, s * 16 : (s + 1) * 16, head(h)] = value[s * TOK + t * 16 : s * TOK + (t + 1) * 16]
    me = lax.axis_index("tp")
    if TERMS_PP:
        rows = jnp.concatenate([att[relative(me, r)] for r in range(NT)], axis=0)
    else:
        rows = att[...].reshape(2 * TOK, 256)
    for i in range(8):
        cols = slice(i * 512, (i + 1) * 512)
        terms = jnp.dot(rows, w_ref[:, cols], preferred_element_type=jnp.float32).astype(jnp.bfloat16)
        if TERMS_PP:
            for r in range(NT):
                refs[r][:, cols] = terms[r * 32 : (r + 1) * 32]
        else:
            refs[0][:, :, cols] = terms.reshape(NT, 32, 512)


def output(mine, far, w_out):
    shapes = (struct(32, D),) * NT if TERMS_PP else (struct(NT, 32, D),)
    return pl.pallas_call(
        output_kernel,
        out_shape=shapes,
        in_specs=[VMEM, VMEM, VMEM],
        out_specs=(VMEM,) * len(shapes),
        scratch_shapes=[pltpu.VMEM((NT, 32, 256), jnp.bfloat16)],
        compiler_params=params(),
        cost_estimate=cost(4, 1 << 29),
        name="terms",
    )(mine, far, w_out)


def sum_kernel(*refs):
    clean_ref, noisy_ref = refs[-2:]
    blocks = refs[:-2]
    total = 0.0
    for t in range(NT):
        block = blocks[t][...] if TERMS_PP else blocks[0][t]
        total = total + block.astype(jnp.float32)
    clean_ref[...] = total[:16].astype(jnp.bfloat16)
    noisy_ref[...] = total[16:].astype(jnp.bfloat16)


def sum_terms(blocks):
    tile = 1024
    if TERMS_PP:
        specs = [pl.BlockSpec((32, tile), lambda i: (0, i))] * NT
    else:
        specs = [pl.BlockSpec((NT, 32, tile), lambda i: (0, 0, i))]
    return pl.pallas_call(
        sum_kernel,
        grid=(D // tile,),
        out_shape=(struct(16, D), struct(16, D)),
        in_specs=specs,
        out_specs=(pl.BlockSpec((16, tile), lambda i: (0, i)),) * 2,
        compiler_params=params(),
        cost_estimate=cost(2),
    )(*blocks)


def ctx_perm(move):
    pairs = []
    for y in range(2):
        for z in range(NZ):
            for c in range(2):
                target = move(y, z, c)
                if target is not None:
                    ty, tz, tc = target
                    pairs.append((y * 16 + z * 2 + c, ty * 16 + tz * 2 + tc))
    return pairs


def ctx_move(x, move):
    return lax.ppermute(x, "ctx", ctx_perm(move))


def swap(x):
    return ctx_move(x, lambda y, z, c: (y, z, 1 - c))


def tp_move(x, r):
    return lax.ppermute(x, "tp", [(i, relative(i, r)) for i in range(NT)])


def tables(positions):
    half = HEAD_DIM // 2
    freqs = ROPE_BASE ** (-2.0 * jnp.arange(half).astype(jnp.float32) / HEAD_DIM)
    angles = positions.astype(jnp.float32)[:, None] * freqs[None, :]
    cosine, sine = jnp.cos(angles), jnp.sin(angles)
    return jnp.concatenate([cosine, cosine], 1), jnp.concatenate([-sine, sine], 1)


def layer(tokens, flags, mask_embed, gain, wq, wk, wv, w_out, block_mask):
    ctx = lax.axis_index("ctx")
    cosine, sine = tables(ctx * TOK + jnp.arange(TOK, dtype=jnp.int32))
    blocks = jnp.arange(block_mask.shape[0], dtype=jnp.int32)
    table = jnp.stack(
        [
            blocks + 1 - jnp.sum(block_mask % 2, axis=1),
            blocks - jnp.sum(block_mask // 2, axis=1),
        ]
    ).astype(jnp.int32)

    rows, mask_row = norm(tokens, flags, mask_embed, gain)
    partner = tp_move(rows, 4)
    gathered = [rows] + [tp_move(rows, 4 - r) for r in (1, 2, 3)]
    gathered += [partner] + [tp_move(partner, 4 - r) for r in (1, 2, 3)]
    w, masked = load_weights(mask_row, wq, wk, wv)
    kv, kvn, all_rows = project_keys(gathered, w, masked, cosine, sine)

    pieces = [kv]
    for s in range(1, NZ):
        pieces.append(ctx_move(kv, lambda y, z, c: (y, (z + s) % NZ, c)))
    q = project_queries(all_rows, w, masked, cosine, sine)
    q_far = ctx_move(q, lambda y, z, c: (0, z, c) if y == 1 else None)
    q_other = swap(q)
    q_far_other = swap(q_far)

    far, far_other = attend(table, q_far, q_far_other, pieces)
    far = merge_cores(far, swap(far_other))
    returned = ctx_move(far, lambda y, z, c: (1, z, c) if y == 0 else None)
    mine, other = attend(table, q, q_other, pieces, kvn, far)
    mine = merge_cores(mine, swap(other))
    terms = list(output(mine, returned, w_out))
    if TERMS_PP:
        for r in range(1, NT):
            terms[r] = tp_move(terms[r], r)
    else:
        terms = [lax.all_to_all(terms[0], "tp", 0, 0)]
    return sum_terms(terms)


def solution(mesh):
    return jax.shard_map(
        layer,
        mesh=mesh,
        in_specs=(
            P(("ctx", "tp"), None),
            P(("ctx", "tp")),
            P(),
            P(),
            P(None, "tp"),
            P(None, "tp"),
            P(None, "tp"),
            P("tp", None),
            P(),
        ),
        out_specs=(P(("ctx", "tp"), None), P(("ctx", "tp"), None)),
        check_vma=False,
    )
```

time: 278 us -> 109 us (0.39)
  waiting for transfers between devices: 171 us -> 16.3 us
  starting transfers between devices: 0.3 us -> 37.8 us
  local copies, waits for them, and re-layouts: 41.2 us -> 7.72 us
  matrix products: 21.5 us -> 0 us
  blocking collectives: 13.7 us -> 31.6 us
  between operations: 15.4 us -> 0.86 us
  Pallas kernels: 0 us -> 13.5 us
  other arithmetic: 13.3 us -> 0.57 us
    all_gather x2 -> x0, waiting for transfers between devices: 88.7 us -> none  [the longest x1 57.1 us: local(): piece = lax.all_gather(key_values, 'ctx', axis=1, tiled=True)]
    unnamed x4 -> x0, waiting for transfers between devices: 82.7 us -> none
    ppermute x0 -> x20, starting transfers between devices: none -> 37.8 us  [the longest x13 26.2 us: ctx_move(): return lax.ppermute(x, 'ctx', ctx_perm(move))]
    all_to_all x0 -> x1, blocking collectives: none -> 31.6 us  [layer(): terms = [lax.all_to_all(terms[0], 'tp', 0, 0)]]
    dot_general x13 -> x0, matrix products: 21.5 us -> none  [the longest x3 7.17 us: project(): clean = jnp.dot(gathered, weight, preferred_element_type=jnp.float32)]
    ppermute x0 -> x20, waiting for transfers between devices: none -> 16.3 us  [the longest x13 13.8 us: ctx_move(): return lax.ppermute(x, 'ctx', ctx_perm(move))]
    unnamed x1 -> x0, blocking collectives: 13.7 us -> none
    pallas_call x0 -> x10, Pallas kernels: none -> 13.5 us  [the longest x2 5.96 us: attend(): pl.pallas_call(kernel, out_shape=(struct(2 * TOK, 384), struct(2 * TOK, 3...]
  transfers between devices with their start and end apart: 3 -> 20, of which waited for: 3 -> 9; matrix products, arithmetic and copies ran while one was open for 6% -> 1% of each run, Pallas kernels for 0% -> 2%
where the time goes in v1:
time: 109 us; the launch traced here: 108 us
  starting transfers between devices  37.8 us (35%)
  blocking collectives  31.6 us (29%)
  waiting for transfers between devices  16.3 us (15%)
  Pallas kernels  13.5 us (12%)
  local copies, waits for them, and re-layouts  7.72 us (7%)
    all_to_all x1, blocking collectives, layer(): terms = [lax.all_to_all(terms[0], 'tp', 0, 0)]  31.6 us
    ppermute x13, starting transfers between devices, ctx_move(): return lax.ppermute(x, 'ctx', ctx_perm(move))  26.2 us
    ppermute x13, waiting for transfers between devices, ctx_move(): return lax.ppermute(x, 'ctx', ctx_perm(move))  13.8 us
    ppermute x7, starting transfers between devices, tp_move(): return lax.ppermute(x, 'tp', [(i, relative(i, r)) for i in range(NT)])  11.7 us
    unnamed x18, local copies, waits for them, and re-layouts  7.72 us
    pallas_call x2, Pallas kernels, attend(): pl.pallas_call(kernel, out_shape=(struct(2 * TOK, 384), struct(2 * TOK, 3...  5.96 us
    ppermute x7, waiting for transfers between devices, tp_move(): return lax.ppermute(x, 'tp', [(i, relative(i, r)) for i in range(NT)])  2.6 us
  transfers between devices with their start and end apart: 20, of which 9 were waited for; matrix products, arithmetic and copies ran while one was open for 1% of the time, Pallas kernels for 2%

profile of v1, /device:TPU:32, one launch (start us, length us, event | category | flops | bytes accessed | tf_op | source)
XLA Modules:
  0.0 108.4 jit_solution(18383898267472157810)
XLA Ops:
  0.6 0.9 copy-done.4
  3.6 0.9 norm.1
  4.5 3.3 %collective-permute-start.3 = (bf16[16,4224]{1,0:T(8,128)(2,1)S(1)}, bf16[16,4224]{1,0:T(8,128)(2,1)S(1)}, u32[]{:S(2)}, u32[]{:S(2)}) collective-permute-start(bf16[16,4224]{1,0:T(8,128)(2,1)S(1)} %get-tuple-element.13.refs_0_), channel_id=1, source_target_pairs={{0,4},{1,5},{2,6},{3,7},{4,0},{5,1},{6,2},{7,3},{8,12},{9,13},{10,... | collective-permute-start | bytes 405512 | tf_op jit(solution)/shard_map/ppermute | solution.py:431
  7.7 2.8 %collective-permute-start = (bf16[16,4224]{1,0:T(8,128)(2,1)S(1)}, bf16[16,4224]{1,0:T(8,128)(2,1)S(1)}, u32[]{:S(2)}, u32[]{:S(2)}) collective-permute-start(bf16[16,4224]{1,0:T(8,128)(2,1)S(1)} %get-tuple-element.13.refs_0_), channel_id=1, source_target_pairs={{0,3},{1,0},{2,1},{3,2},{4,7},{5,4},{6,5},{7,6},{8,11},{9,8},{10,9... | collective-permute-start | bytes 405512 | tf_op jit(solution)/shard_map/ppermute | solution.py:431
  10.5 0.8 collective-permute-start.1
  11.3 0.9 collective-permute-start.2
  12.2 2.4 %collective-permute-start.4 = (bf16[16,4224]{1,0:T(8,128)(2,1)S(1)}, bf16[16,4224]{1,0:T(8,128)(2,1)S(1)}, u32[]{:S(2)}, u32[]{:S(2)}) collective-permute-start(bf16[16,4224]{1,0:T(8,128)(2,1)S(1)} %collective-permute-done.3.refs_4_), channel_id=1, source_target_pairs={{0,3},{1,0},{2,1},{3,2},{4,7},{5,4},{6,5},{7,6},{8,11},{9,8},{10,9... | collective-permute-start | bytes 405512 | tf_op jit(solution)/shard_map/ppermute | solution.py:431
  14.6 1.5 %collective-permute-start.5 = (bf16[16,4224]{1,0:T(8,128)(2,1)S(1)}, bf16[16,4224]{1,0:T(8,128)(2,1)S(1)}, u32[]{:S(2)}, u32[]{:S(2)}) collective-permute-start(bf16[16,4224]{1,0:T(8,128)(2,1)S(1)} %collective-permute-done.3.refs_4_), channel_id=1, source_target_pairs={{0,2},{1,3},{2,0},{3,1},{4,6},{5,7},{6,4},{7,5},{8,10},{9,11},{10,... | collective-permute-start | bytes 405512 | tf_op jit(solution)/shard_map/ppermute | solution.py:431
  16.2 0.8 collective-permute-done.refs_1_
  17.3 1.6 %copy-done = bf16[4096,256]{1,0:T(8,128)(2,1)S(1)} copy-done((bf16[4096,256]{1,0:T(8,128)(2,1)S(1)}, bf16[4096,256]{1,0:T(8,128)(2,1)}, u32[]{:S(2)}) %copy-start) | copy-done | bytes 2097176
  18.9 1.6 %copy-done.1 = bf16[4096,256]{1,0:T(8,128)(2,1)S(1)} copy-done((bf16[4096,256]{1,0:T(8,128)(2,1)S(1)}, bf16[4096,256]{1,0:T(8,128)(2,1)}, u32[]{:S(2)}) %copy-start.1) | copy-done | bytes 2097176
  20.5 1.6 %copy-done.2 = bf16[4096,256]{1,0:T(8,128)(2,1)S(1)} copy-done((bf16[4096,256]{1,0:T(8,128)(2,1)S(1)}, bf16[4096,256]{1,0:T(8,128)(2,1)}, u32[]{:S(2)}) %copy-start.2) | copy-done | bytes 2097176
  22.1 1.5 %weights.1 = (bf16[4096,768]{1,0:T(8,128)(2,1)S(1)}, f32[8,768]{1,0:T(8,128)S(1)}) custom-call(bf16[16,4096]{1,0:T(8,128)(2,1)S(1)} %get-tuple-element.14.mask_ref, bf16[4096,256]{1,0:T(8,128)(2,1)S(1)} %copy-done, bf16[4096,256]{1,0:T(8,128)(2,1)S(1)} %copy-done.1, bf16[4096,256]{1,0:T(8,128)(2,1)S(1)} %copy-done.2), custom_call_target="tpu_custom_call" | custom-call | flops 1048576 | bytes 12582912 | tf_op jit(solution)/shard_map/weights/pallas_call | solution.py:119
  24.0 1.4 %collective-permute-done.6.refs_7_ = bf16[16,4224]{1,0:T(8,128)(2,1)S(1)} collective-permute-done((bf16[16,4224]{1,0:T(8,128)(2,1)S(1)}, bf16[16,4224]{1,0:T(8,128)(2,1)S(1)}, u32[]{:S(2)}, u32[]{:S(2)}) %collective-permute-start.6) | collective-permute-done | bytes 135200 | tf_op jit(solution)/shard_map/ppermute | solution.py:431
  25.5 0.9 keys.1
  26.9 1.3 %collective-permute-start.15 = (bf16[256,256]{1,0:T(8,128)(2,1)S(1)}, bf16[256,256]{1,0:T(8,128)(2,1)S(1)}, u32[]{:S(2)}, u32[]{:S(2)}) collective-permute-start(bf16[256,256]{1,0:T(8,128)(2,1)S(1)} %queries.1.refs_1_), channel_id=1, source_target_pairs={{128,0},{136,8},{144,16},{152,24},{160,32},{168,40},{176,48},{184,... | collective-permute-start | bytes 393224 | tf_op jit(solution)/shard_map/ppermute | solution.py:423
  28.2 5.9 %collective-permute-start.10 = (bf16[128,512]{1,0:T(8,128)(2,1)S(1)}, bf16[128,512]{1,0:T(8,128)(2,1)S(1)}, u32[]{:S(2)}, u32[]{:S(2)}) collective-permute-start(bf16[128,512]{1,0:T(8,128)(2,1)S(1)} %get-tuple-element.18.refs_3_), channel_id=1, source_target_pairs={{0,48},{8,56},{16,64},{24,72},{32,80},{40,88},{48,96},{56,104},{64... | collective-permute-start | bytes 393224 | tf_op jit(solution)/shard_map/ppermute | solution.py:423
  34.7 4.9 %collective-permute-start.12 = (bf16[128,512]{1,0:T(8,128)(2,1)S(1)}, bf16[128,512]{1,0:T(8,128)(2,1)S(1)}, u32[]{:S(2)}, u32[]{:S(2)}) collective-permute-start(bf16[128,512]{1,0:T(8,128)(2,1)S(1)} %get-tuple-element.18.refs_3_), channel_id=1, source_target_pairs={{0,80},{8,88},{16,96},{24,104},{32,112},{40,120},{48,0},{56,8},{64... | collective-permute-start | bytes 393224 | tf_op jit(solution)/shard_map/ppermute | solution.py:423
  39.9 1.1 %collective-permute-start.14 = (bf16[128,512]{1,0:T(8,128)(2,1)S(1)}, bf16[128,512]{1,0:T(8,128)(2,1)S(1)}, u32[]{:S(2)}, u32[]{:S(2)}) collective-permute-start(bf16[128,512]{1,0:T(8,128)(2,1)S(1)} %get-tuple-element.18.refs_3_), channel_id=1, source_target_pairs={{0,112},{8,120},{16,0},{24,8},{32,16},{40,24},{48,32},{56,40},{64,... | collective-permute-start | bytes 393224 | tf_op jit(solution)/shard_map/ppermute | solution.py:423
  40.9 1.9 %collective-permute-done.10.refs_6_ = bf16[128,512]{1,0:T(8,128)(2,1)S(1)} collective-permute-done((bf16[128,512]{1,0:T(8,128)(2,1)S(1)}, bf16[128,512]{1,0:T(8,128)(2,1)S(1)}, u32[]{:S(2)}, u32[]{:S(2)}) %collective-permute-start.10) | collective-permute-done | bytes 131104 | tf_op jit(solution)/shard_map/ppermute | solution.py:423
  42.8 4.1 %collective-permute-start.8 = (bf16[128,512]{1,0:T(8,128)(2,1)S(1)}, bf16[128,512]{1,0:T(8,128)(2,1)S(1)}, u32[]{:S(2)}, u32[]{:S(2)}) collective-permute-start(bf16[128,512]{1,0:T(8,128)(2,1)S(1)} %get-tuple-element.18.refs_3_), channel_id=1, source_target_pairs={{0,16},{8,24},{16,32},{24,40},{32,48},{40,56},{48,64},{56,72},{64,... | collective-permute-start | bytes 393224 | tf_op jit(solution)/shard_map/ppermute | solution.py:423
  47.2 5.0 %collective-permute-start.9 = (bf16[128,512]{1,0:T(8,128)(2,1)S(1)}, bf16[128,512]{1,0:T(8,128)(2,1)S(1)}, u32[]{:S(2)}, u32[]{:S(2)}) collective-permute-start(bf16[128,512]{1,0:T(8,128)(2,1)S(1)} %get-tuple-element.18.refs_3_), channel_id=1, source_target_pairs={{0,32},{8,40},{16,48},{24,56},{32,64},{40,72},{48,80},{56,88},{64,... | collective-permute-start | bytes 393224 | tf_op jit(solution)/shard_map/ppermute | solution.py:423
  52.2 3.0 %collective-permute-done.12.refs_8_ = bf16[128,512]{1,0:T(8,128)(2,1)S(1)} collective-permute-done((bf16[128,512]{1,0:T(8,128)(2,1)S(1)}, bf16[128,512]{1,0:T(8,128)(2,1)S(1)}, u32[]{:S(2)}, u32[]{:S(2)}) %collective-permute-start.12) | collective-permute-done | bytes 131104 | tf_op jit(solution)/shard_map/ppermute | solution.py:423
  55.2 3.5 %collective-permute-done.14.refs_10_ = bf16[128,512]{1,0:T(8,128)(2,1)S(1)} collective-permute-done((bf16[128,512]{1,0:T(8,128)(2,1)S(1)}, bf16[128,512]{1,0:T(8,128)(2,1)S(1)}, u32[]{:S(2)}, u32[]{:S(2)}) %collective-permute-start.14) | collective-permute-done | bytes 131104 | tf_op jit(solution)/shard_map/ppermute | solution.py:423
  58.8 2.8 %attend_far.1 = (bf16[256,384]{1,0:T(8,128)(2,1)S(1)}, bf16[256,384]{1,0:T(8,128)(2,1)S(1)}) custom-call(s32[2,128]{1,0:T(2,128)S(1)} %pad_add_fusion.refs_0_, bf16[256,256]{1,0:T(8,128)(2,1)S(1)} %collective-permute-done.15.refs_1_, bf16[256,256]{1,0:T(8,128)(2,1)S(1)} %collective-permute-done.16.refs_2_, bf16[128,512]{1,0:T(8,128)(2,1)S(1)} %get-tuple-element.18.refs_3_, ...), custom_call_target="tpu_custom_call" | custom-call | flops 536870912 | bytes 4194304 | tf_op jit(solution)/shard_map/attend_far/pallas_call | solution.py:300
  62.2 0.9 collective-permute-done.17.swap_ref
  63.7 3.1 %attend_near.1 = (bf16[256,384]{1,0:T(8,128)(2,1)S(1)}, bf16[256,384]{1,0:T(8,128)(2,1)S(1)}) custom-call(s32[2,128]{1,0:T(2,128)S(1)} %pad_add_fusion.refs_0_, bf16[256,256]{1,0:T(8,128)(2,1)S(1)} %queries.1.refs_1_, bf16[256,256]{1,0:T(8,128)(2,1)S(1)} %collective-permute-done.7.refs_2_, bf16[128,512]{1,0:T(8,128)(2,1)S(1)} %get-tuple-element.18.refs_3_, ...), custom_call_target="tpu_custom_call" | custom-call | flops 536870912 | bytes 4194304 | tf_op jit(solution)/shard_map/attend_near/pallas_call | solution.py:300
  67.1 2.4 %collective-permute-start.19 = (bf16[256,384]{1,0:T(8,128)(2,1)S(1)}, bf16[256,384]{1,0:T(8,128)(2,1)S(1)}, u32[]{:S(2)}, u32[]{:S(2)}) collective-permute-start(bf16[256,384]{1,0:T(8,128)(2,1)S(1)} %shard_map.104.refs_12_), channel_id=1, source_target_pairs={{0,128},{8,136},{16,144},{24,152},{32,160},{40,168},{48,176},{56,1... | collective-permute-start | bytes 589832 | tf_op jit(solution)/shard_map/ppermute | solution.py:423
  70.0 4.1 %collective-permute-done.19.far_ref = bf16[256,384]{1,0:T(8,128)(2,1)S(1)} collective-permute-done((bf16[256,384]{1,0:T(8,128)(2,1)S(1)}, bf16[256,384]{1,0:T(8,128)(2,1)S(1)}, u32[]{:S(2)}, u32[]{:S(2)}) %collective-permute-start.19) | collective-permute-done | bytes 196640 | tf_op jit(solution)/shard_map/ppermute | solution.py:423
  74.1 1.1 %terms.1 = bf16[8,32,4096]{2,1,0:T(8,128)(2,1)S(1)} custom-call(bf16[256,384]{1,0:T(8,128)(2,1)S(1)} %shard_map.105.self_ref, bf16[256,384]{1,0:T(8,128)(2,1)S(1)} %collective-permute-done.19.far_ref, bf16[256,4096]{1,0:T(8,128)(2,1)S(1)} %copy-done.3), custom_call_target="tpu_custom_call" | custom-call | flops 536870912 | bytes 4194304 | tf_op jit(solution)/shard_map/terms/pallas_call | solution.py:370
  75.2 31.6 %all_to_all.5.refs_0_ = bf16[8,32,4096]{2,1,0:T(8,128)(2,1)S(1)} all-to-all(bf16[8,32,4096]{2,1,0:T(8,128)(2,1)S(1)} %terms.1), channel_id=1, replica_groups=mesh['ctx'=32,'tp'=8] {'tp'}, dimensions={0} | all-to-all | bytes 4194304 | tf_op jit(solution)/shard_map/all_to_all | solution.py:478
  106.8 1.6 %shard_map.106 = (bf16[16,4096]{1,0:T(8,128)(2,1)}, bf16[16,4096]{1,0:T(8,128)(2,1)}) custom-call(bf16[8,32,4096]{2,1,0:T(8,128)(2,1)S(1)} %all_to_all.5.refs_0_), custom_call_target="tpu_custom_call" | custom-call | flops 1048576 | bytes 2097152 | tf_op jit(solution)/shard_map/pallas_call | solution.py:399
  (44 shorter events, 6.3 us)
Async XLA Ops:
  0.6 0.9 copy-start.4
  1.5 0.7 copy-start.5
  2.2 0.7 copy-start.6
  2.9 0.7 copy-start.7
  4.5 7.7 %collective-permute-start.3 = (bf16[16,4224]{1,0:T(8,128)(2,1)S(1)}, bf16[16,4224]{1,0:T(8,128)(2,1)S(1)}, u32[]{:S(2)}, u32[]{:S(2)}) collective-permute-start(bf16[16,4224]{1,0:T(8,128)(2,1)S(1)} %get-tuple-element.13.refs_0_), channel_id=1, source_target_pairs={{0,4},{1,5},{2,6},{3,7},{4,0},{5,1},{6,2},{7,3},{8,12},{9,13},{10,... | collective-permute-start | bytes 405512 | tf_op jit(solution)/shard_map/ppermute | solution.py:431
  7.7 9.3 %collective-permute-start = (bf16[16,4224]{1,0:T(8,128)(2,1)S(1)}, bf16[16,4224]{1,0:T(8,128)(2,1)S(1)}, u32[]{:S(2)}, u32[]{:S(2)}) collective-permute-start(bf16[16,4224]{1,0:T(8,128)(2,1)S(1)} %get-tuple-element.13.refs_0_), channel_id=1, source_target_pairs={{0,3},{1,0},{2,1},{3,2},{4,7},{5,4},{6,5},{7,6},{8,11},{9,8},{10,9... | collective-permute-start | bytes 405512 | tf_op jit(solution)/shard_map/ppermute | solution.py:431
  10.5 13.2 %collective-permute-start.1 = (bf16[16,4224]{1,0:T(8,128)(2,1)S(1)}, bf16[16,4224]{1,0:T(8,128)(2,1)S(1)}, u32[]{:S(2)}, u32[]{:S(2)}) collective-permute-start(bf16[16,4224]{1,0:T(8,128)(2,1)S(1)} %get-tuple-element.13.refs_0_), channel_id=1, source_target_pairs={{0,2},{1,3},{2,0},{3,1},{4,6},{5,7},{6,4},{7,5},{8,10},{9,11},{10,... | collective-permute-start | bytes 405512 | tf_op jit(solution)/shard_map/ppermute | solution.py:431
  11.3 12.4 %collective-permute-start.2 = (bf16[16,4224]{1,0:T(8,128)(2,1)S(1)}, bf16[16,4224]{1,0:T(8,128)(2,1)S(1)}, u32[]{:S(2)}, u32[]{:S(2)}) collective-permute-start(bf16[16,4224]{1,0:T(8,128)(2,1)S(1)} %get-tuple-element.13.refs_0_), channel_id=1, source_target_pairs={{0,1},{1,2},{2,3},{3,0},{4,5},{5,6},{6,7},{7,4},{8,9},{9,10},{10,1... | collective-permute-start | bytes 405512 | tf_op jit(solution)/shard_map/ppermute | solution.py:431
  12.2 11.5 %collective-permute-start.4 = (bf16[16,4224]{1,0:T(8,128)(2,1)S(1)}, bf16[16,4224]{1,0:T(8,128)(2,1)S(1)}, u32[]{:S(2)}, u32[]{:S(2)}) collective-permute-start(bf16[16,4224]{1,0:T(8,128)(2,1)S(1)} %collective-permute-done.3.refs_4_), channel_id=1, source_target_pairs={{0,3},{1,0},{2,1},{3,2},{4,7},{5,4},{6,5},{7,6},{8,11},{9,8},{10,9... | collective-permute-start | bytes 405512 | tf_op jit(solution)/shard_map/ppermute | solution.py:431
  14.6 9.4 %collective-permute-start.5 = (bf16[16,4224]{1,0:T(8,128)(2,1)S(1)}, bf16[16,4224]{1,0:T(8,128)(2,1)S(1)}, u32[]{:S(2)}, u32[]{:S(2)}) collective-permute-start(bf16[16,4224]{1,0:T(8,128)(2,1)S(1)} %collective-permute-done.3.refs_4_), channel_id=1, source_target_pairs={{0,2},{1,3},{2,0},{3,1},{4,6},{5,7},{6,4},{7,5},{8,10},{9,11},{10,... | collective-permute-start | bytes 405512 | tf_op jit(solution)/shard_map/ppermute | solution.py:431
  17.0 8.5 %collective-permute-start.6 = (bf16[16,4224]{1,0:T(8,128)(2,1)S(1)}, bf16[16,4224]{1,0:T(8,128)(2,1)S(1)}, u32[]{:S(2)}, u32[]{:S(2)}) collective-permute-start(bf16[16,4224]{1,0:T(8,128)(2,1)S(1)} %collective-permute-done.3.refs_4_), channel_id=1, source_target_pairs={{0,1},{1,2},{2,3},{3,0},{4,5},{5,6},{6,7},{7,4},{8,9},{9,10},{10,1... | collective-permute-start | bytes 405512 | tf_op jit(solution)/shard_map/ppermute | solution.py:431
  17.3 1.6 %copy-start = (bf16[4096,256]{1,0:T(8,128)(2,1)S(1)}, bf16[4096,256]{1,0:T(8,128)(2,1)}, u32[]{:S(2)}) copy-start(bf16[4096,256]{1,0:T(8,128)(2,1)} %wq_hbm.1) | copy-start | bytes 6291460
  18.9 1.6 %copy-start.1 = (bf16[4096,256]{1,0:T(8,128)(2,1)S(1)}, bf16[4096,256]{1,0:T(8,128)(2,1)}, u32[]{:S(2)}) copy-start(bf16[4096,256]{1,0:T(8,128)(2,1)} %wk_hbm.1) | copy-start | bytes 6291460
  20.5 1.6 %copy-start.2 = (bf16[4096,256]{1,0:T(8,128)(2,1)S(1)}, bf16[4096,256]{1,0:T(8,128)(2,1)}, u32[]{:S(2)}) copy-start(bf16[4096,256]{1,0:T(8,128)(2,1)} %wv_hbm.1) | copy-start | bytes 6291460
  26.3 13.3 %copy-start.8 = (s32[128,128]{1,0:T(8,128)S(1)}, s32[128,128]{1,0:T(8,128)}, u32[]{:S(2)}) copy-start(s32[128,128]{1,0:T(8,128)} %param.17) | copy-start | bytes 196612
  26.9 12.9 %collective-permute-start.15 = (bf16[256,256]{1,0:T(8,128)(2,1)S(1)}, bf16[256,256]{1,0:T(8,128)(2,1)S(1)}, u32[]{:S(2)}, u32[]{:S(2)}) collective-permute-start(bf16[256,256]{1,0:T(8,128)(2,1)S(1)} %queries.1.refs_1_), channel_id=1, source_target_pairs={{128,0},{136,8},{144,16},{152,24},{160,32},{168,40},{176,48},{184,... | collective-permute-start | bytes 393224 | tf_op jit(solution)/shard_map/ppermute | solution.py:423
  28.2 14.6 %collective-permute-start.10 = (bf16[128,512]{1,0:T(8,128)(2,1)S(1)}, bf16[128,512]{1,0:T(8,128)(2,1)S(1)}, u32[]{:S(2)}, u32[]{:S(2)}) collective-permute-start(bf16[128,512]{1,0:T(8,128)(2,1)S(1)} %get-tuple-element.18.refs_3_), channel_id=1, source_target_pairs={{0,48},{8,56},{16,64},{24,72},{32,80},{40,88},{48,96},{56,104},{64... | collective-permute-start | bytes 393224 | tf_op jit(solution)/shard_map/ppermute | solution.py:423
  34.1 13.1 %collective-permute-start.11 = (bf16[128,512]{1,0:T(8,128)(2,1)S(1)}, bf16[128,512]{1,0:T(8,128)(2,1)S(1)}, u32[]{:S(2)}, u32[]{:S(2)}) collective-permute-start(bf16[128,512]{1,0:T(8,128)(2,1)S(1)} %get-tuple-element.18.refs_3_), channel_id=1, source_target_pairs={{0,64},{8,72},{16,80},{24,88},{32,96},{40,104},{48,112},{56,120},{... | collective-permute-start | bytes 393224 | tf_op jit(solution)/shard_map/ppermute | solution.py:423
  34.7 20.5 %collective-permute-start.12 = (bf16[128,512]{1,0:T(8,128)(2,1)S(1)}, bf16[128,512]{1,0:T(8,128)(2,1)S(1)}, u32[]{:S(2)}, u32[]{:S(2)}) collective-permute-start(bf16[128,512]{1,0:T(8,128)(2,1)S(1)} %get-tuple-element.18.refs_3_), channel_id=1, source_target_pairs={{0,80},{8,88},{16,96},{24,104},{32,112},{40,120},{48,0},{56,8},{64... | collective-permute-start | bytes 393224 | tf_op jit(solution)/shard_map/ppermute | solution.py:423
  39.8 15.5 %collective-permute-start.13 = (bf16[128,512]{1,0:T(8,128)(2,1)S(1)}, bf16[128,512]{1,0:T(8,128)(2,1)S(1)}, u32[]{:S(2)}, u32[]{:S(2)}) collective-permute-start(bf16[128,512]{1,0:T(8,128)(2,1)S(1)} %get-tuple-element.18.refs_3_), channel_id=1, source_target_pairs={{0,96},{8,104},{16,112},{24,120},{32,0},{40,8},{48,16},{56,24},{64... | collective-permute-start | bytes 393224 | tf_op jit(solution)/shard_map/ppermute | solution.py:423
  39.9 18.9 %collective-permute-start.14 = (bf16[128,512]{1,0:T(8,128)(2,1)S(1)}, bf16[128,512]{1,0:T(8,128)(2,1)S(1)}, u32[]{:S(2)}, u32[]{:S(2)}) collective-permute-start(bf16[128,512]{1,0:T(8,128)(2,1)S(1)} %get-tuple-element.18.refs_3_), channel_id=1, source_target_pairs={{0,112},{8,120},{16,0},{24,8},{32,16},{40,24},{48,32},{56,40},{64,... | collective-permute-start | bytes 393224 | tf_op jit(solution)/shard_map/ppermute | solution.py:423
  42.8 16.0 %collective-permute-start.8 = (bf16[128,512]{1,0:T(8,128)(2,1)S(1)}, bf16[128,512]{1,0:T(8,128)(2,1)S(1)}, u32[]{:S(2)}, u32[]{:S(2)}) collective-permute-start(bf16[128,512]{1,0:T(8,128)(2,1)S(1)} %get-tuple-element.18.refs_3_), channel_id=1, source_target_pairs={{0,16},{8,24},{16,32},{24,40},{32,48},{40,56},{48,64},{56,72},{64,... | collective-permute-start | bytes 393224 | tf_op jit(solution)/shard_map/ppermute | solution.py:423
  47.2 11.6 %collective-permute-start.9 = (bf16[128,512]{1,0:T(8,128)(2,1)S(1)}, bf16[128,512]{1,0:T(8,128)(2,1)S(1)}, u32[]{:S(2)}, u32[]{:S(2)}) collective-permute-start(bf16[128,512]{1,0:T(8,128)(2,1)S(1)} %get-tuple-element.18.refs_3_), channel_id=1, source_target_pairs={{0,32},{8,40},{16,48},{24,56},{32,64},{40,72},{48,80},{56,88},{64,... | collective-permute-start | bytes 393224 | tf_op jit(solution)/shard_map/ppermute | solution.py:423
  55.2 3.6 %collective-permute-start.16 = (bf16[256,256]{1,0:T(8,128)(2,1)S(1)}, bf16[256,256]{1,0:T(8,128)(2,1)S(1)}, u32[]{:S(2)}, u32[]{:S(2)}) collective-permute-start(bf16[256,256]{1,0:T(8,128)(2,1)S(1)} %collective-permute-done.15.refs_1_), channel_id=1, source_target_pairs={{0,8},{8,0},{16,24},{24,16},{32,40},{40,32},{48,56},{56,48},{64,72... | collective-permute-start | bytes 393224 | tf_op jit(solution)/shard_map/ppermute | solution.py:423
  55.2 18.9 %copy-start.3 = (bf16[256,4096]{1,0:T(8,128)(2,1)S(1)}, bf16[256,4096]{1,0:T(8,128)(2,1)}, u32[]{:S(2)}) copy-start(bf16[256,4096]{1,0:T(8,128)(2,1)} %w_ref.1) | copy-start | bytes 6291460
  61.6 1.5 %collective-permute-start.17 = (bf16[256,384]{1,0:T(8,128)(2,1)S(1)}, bf16[256,384]{1,0:T(8,128)(2,1)S(1)}, u32[]{:S(2)}, u32[]{:S(2)}) collective-permute-start(bf16[256,384]{1,0:T(8,128)(2,1)S(1)} %get-tuple-element.21), channel_id=1, source_target_pairs={{0,8},{8,0},{16,24},{24,16},{32,40},{40,32},{48,56},{56,48},{64,72... | collective-permute-start | bytes 589832 | tf_op jit(solution)/shard_map/ppermute | solution.py:423
  61.7 1.9 %collective-permute-start.7 = (bf16[256,256]{1,0:T(8,128)(2,1)S(1)}, bf16[256,256]{1,0:T(8,128)(2,1)S(1)}, u32[]{:S(2)}, u32[]{:S(2)}) collective-permute-start(bf16[256,256]{1,0:T(8,128)(2,1)S(1)} %queries.1.refs_1_), channel_id=1, source_target_pairs={{0,8},{8,0},{16,24},{24,16},{32,40},{40,32},{48,56},{56,48},{64,72... | collective-permute-start | bytes 393224 | tf_op jit(solution)/shard_map/ppermute | solution.py:423
  66.8 2.6 %collective-permute-start.18 = (bf16[256,384]{1,0:T(8,128)(2,1)S(1)}, bf16[256,384]{1,0:T(8,128)(2,1)S(1)}, u32[]{:S(2)}, u32[]{:S(2)}) collective-permute-start(bf16[256,384]{1,0:T(8,128)(2,1)S(1)} %get-tuple-element.23), channel_id=1, source_target_pairs={{0,8},{8,0},{16,24},{24,16},{32,40},{40,32},{48,56},{56,48},{64,72... | collective-permute-start | bytes 589832 | tf_op jit(solution)/shard_map/ppermute | solution.py:423
  67.1 7.0 %collective-permute-start.19 = (bf16[256,384]{1,0:T(8,128)(2,1)S(1)}, bf16[256,384]{1,0:T(8,128)(2,1)S(1)}, u32[]{:S(2)}, u32[]{:S(2)}) collective-permute-start(bf16[256,384]{1,0:T(8,128)(2,1)S(1)} %shard_map.104.refs_12_), channel_id=1, source_target_pairs={{0,128},{8,136},{16,144},{24,152},{32,160},{40,168},{48,176},{56,1... | collective-permute-start | bytes 589832 | tf_op jit(solution)/shard_map/ppermute | solution.py:423

commit v2 on v1

--- a/solution.py
+++ b/solution.py
@@ -18,7 +18,7 @@
 SCALE2 = HEAD_DIM ** (-0.5) * LOG2E
 HIDDEN = -1e30
 FLOOR = -1e29
-TERMS_PP = False
+TERMS_PP = True
 
 
 VMEM = pl.BlockSpec(memory_space=pltpu.VMEM)
@@ -89,10 +89,10 @@
             pltpu.VMEM((D // 128, 128), jnp.bfloat16),
             pltpu.SemaphoreType.DMA((4,)),
         ],
-        compiler_params=params(),
+        compiler_params=pltpu.CompilerParams(vmem_limit_bytes=16 << 20),
         cost_estimate=cost(1),
         name="norm",
-    )(tokens, flags, mask_embed.reshape(D // 128, 128), gain.reshape(D // 128, 128))
+    )(*(pltpu.with_memory_space_constraint(v, pltpu.HBM) for v in (tokens, flags, mask_embed.reshape(D // 128, 128), gain.reshape(D // 128, 128))))
 
 
 def weights_kernel(mask_ref, wq_hbm, wk_hbm, wv_hbm, w_ref, masked_ref, sems):
@@ -122,10 +122,10 @@
         in_specs=[VMEM, HBM, HBM, HBM],
         out_specs=(VMEM, VMEM),
         scratch_shapes=[pltpu.SemaphoreType.DMA((3, 4))],
-        compiler_params=params(),
+        compiler_params=pltpu.CompilerParams(vmem_limit_bytes=16 << 20),
         cost_estimate=cost(12),
         name="weights",
-    )(mask_row, wq, wk, wv)
+    )(mask_row, *(pltpu.with_memory_space_constraint(w, pltpu.HBM) for w in (wq, wk, wv)))
 
 
 def place():
@@ -211,122 +211,191 @@
     ]
 
 
-def attend_kernel(far, *refs):
-    table_ref, mine_ref, other_ref = refs[:3]
-    kv_refs = refs[3 : 3 + NZ]
-    rest = refs[3 + NZ :]
-    kvn_ref = None if far else rest[0]
-    out_mine, out_other, keys = rest[-3:]
+def unpack(ref):
+    block = ref[...]
+    return [block[:, head(h)].astype(jnp.float32) for h in range(2)], unpack_stats(block[:, 256:])
+
+
+def pack(part, ref):
+    outs, lses = part
+    for h in range(2):
+        ref[:, head(h)] = outs[h].astype(jnp.bfloat16)
+    ref[:, 256:] = pack_stats(lses)
+
+
+def merge(a, b):
+    outs, lses = [], []
+    for h in range(2):
+        peak = jnp.maximum(a[1][h], b[1][h])
+        wa, wb = jnp.exp2(a[1][h] - peak), jnp.exp2(b[1][h] - peak)
+        total = wa + wb
+        outs.append((a[0][h] * wa + b[0][h] * wb) / total)
+        lses.append(peak + jnp.log2(total))
+    return outs, lses
+
+
+TILES = ((0, 0), (2, 0), (2, 1), (1, 0), (1, 1), (3, 0), (3, 1), (4, 0))
+EARLY = TILES[:5]
+LATE = TILES[5:]
+
+
+def tile_block(tile, y, z, c):
+    step, flip = tile
+    source = (z + jnp.where(c == 0, NZ - step, step)) % NZ
+    core = 1 - c if flip else c
+    return (y * 16 + source * 2 + core) * 4
+
+
+def partial(q, keys, tiles, table_ref, yq, cq, near=None):
     y, z, c = place()
-    col = lax.broadcasted_iota(jnp.int32, (1, NZ * TOK), 1)
+    col = lax.broadcasted_iota(jnp.int32, (1, len(tiles) * TOK), 1)
+    key_block = (col % TOK) // BLOCK
+    for i, tile in enumerate(tiles):
+        key_block = jnp.where(col // TOK == i, key_block + tile_block(tile, y, z, c), key_block)
+    part = lax.broadcasted_iota(jnp.int32, (2 * TOK, 1), 0) // BLOCK
+    first = (yq * 16 + z * 2 + cq) * 4
+    low = jnp.zeros((2 * TOK, 1), jnp.int32)
+    high = jnp.zeros((2 * TOK, 1), jnp.int32)
+    for p in range(8):
+        copy, block = p // 4, first + p % 4
+        low = jnp.where(part == p, table_ref[copy, block], low)
+        high = jnp.where(part == p, block - copy, high)
+    visible = (key_block >= low) & (key_block <= high)
+    outs, lses = [], []
+    for h in range(2):
+        qh = q[:, head(h)]
+        scores = lax.dot_general(
+            qh, keys[:, head(h)], (((1,), (1,)), ((), ())), preferred_element_type=jnp.float32
+        ) * SCALE2
+        scores = jnp.where(visible, scores, HIDDEN)
+        peak = jnp.maximum(jnp.max(scores, axis=-1, keepdims=True), FLOOR)
+        if near is not None:
+            kvn_ref, wanted = near
+            own = lax.dot_general(
+                qh[TOK:], kvn_ref[:, head(h)], (((1,), (1,)), ((), ())), preferred_element_type=jnp.float32
+            ) * SCALE2
+            same = (
+                lax.broadcasted_iota(jnp.int32, (TOK, TOK), 0) // BLOCK
+                == lax.broadcasted_iota(jnp.int32, (TOK, TOK), 1) // BLOCK
+            ) & wanted
+            own = jnp.where(same, own, HIDDEN)
+            peak_own = jnp.maximum(peak[TOK:], jnp.max(own, axis=-1, keepdims=True))
+            peak = jnp.concatenate([peak[:TOK], peak_own], axis=0)
+        weights = jnp.exp2(scores - peak)
+        total = jnp.sum(weights, axis=-1, keepdims=True)
+        weighted = jnp.dot(
+            weights.astype(jnp.bfloat16), keys[:, head(2 + h)], preferred_element_type=jnp.float32
+        )
+        if near is not None:
+            wown = jnp.exp2(own - peak_own)
+            total = total + jnp.concatenate(
+                [jnp.zeros((TOK, 1), jnp.float32), jnp.sum(wown, axis=-1, keepdims=True)], axis=0
+            )
+            extra = jnp.dot(
+                wown.astype(jnp.bfloat16), kvn_ref[:, head(2 + h)], preferred_element_type=jnp.float32
+            )
+            weighted = weighted + jnp.concatenate(
+                [jnp.zeros((TOK, HEAD_DIM), jnp.float32), extra], axis=0
+            )
+        some = total > 0.0
+        safe = jnp.where(some, total, 1.0)
+        outs.append(weighted / safe)
+        lses.append(jnp.where(some, peak + jnp.log2(safe), FLOOR))
+    return outs, lses
+
+
+def save(part, ref):
+    outs, lses = part
+    for h in range(2):
+        ref[:, head(h)] = outs[h]
+        ref[:, head(2 + h)] = jnp.broadcast_to(lses[h], (2 * TOK, HEAD_DIM))
+
+
+def saved(ref):
+    return [ref[:, head(h)] for h in range(2)], [ref[:, (2 + h) * 128 : (2 + h) * 128 + 1] for h in range(2)]
+
+
+def early_kernel(table_ref, q_ref, other_ref, far_ref, far_other_ref, own_ref, two_ref, one_ref, kvn_ref,
+                 up_mine, up_other, low_mine, low_other, keys):
+    y, _, c = place()
+    keys[:TOK] = own_ref[0]
+    keys[TOK : 3 * TOK] = two_ref[...].reshape(2 * TOK, 512)
+    keys[3 * TOK :] = one_ref[...].reshape(2 * TOK, 512)
+    tiles = EARLY
+    mine = jnp.where(y == 1, q_ref[...], far_ref[...])
+    other = jnp.where(y == 1, other_ref[...], far_other_ref[...])
+    save(partial(mine, keys, tiles, table_ref, 1, c, (kvn_ref, y == 1)), up_mine)
+    save(partial(other, keys, tiles, table_ref, 1, 1 - c), up_other)
+
+    @pl.when(y == 0)
+    def _():
+        save(partial(q_ref[...], keys, tiles, table_ref, 0, c, (kvn_ref, y == 0)), low_mine)
+        save(partial(other_ref[...], keys, tiles, table_ref, 0, 1 - c), low_other)
+
+    @pl.when(y == 1)
+    def _():
+        low_mine[...] = jnp.zeros_like(low_mine)
+        low_other[...] = jnp.zeros_like(low_other)
+
+
+def early(table, q, other, far, far_other, own, two, one, kvn):
+    return pl.pallas_call(
+        early_kernel,
+        out_shape=(struct(2 * TOK, 512, dtype=jnp.float32),) * 4,
+        in_specs=[SMEM] + [VMEM] * 8,
+        out_specs=(VMEM,) * 4,
+        scratch_shapes=[pltpu.VMEM((len(EARLY) * TOK, 512), jnp.bfloat16)],
+        compiler_params=params(),
+        cost_estimate=cost(4, 1 << 29),
+        name="early",
+    )(table, q, other, far, far_other, own, two, one, kvn)
+
+
+def late_kernel(line, table_ref, q_ref, other_ref, far_ref, far_other_ref, three_ref, half_ref, mine_ref, swap_ref, _,
+                out_mine, out_other, keys):
+    y, _, c = place()
 
     def work():
-        for s in range(NZ):
-            keys[s * TOK : (s + 1) * TOK, :] = kv_refs[s][...]
-        source = (z - col // TOK) & (NZ - 1)
-        key_block = (y * 16 + source * 2 + c) * 4 + (col % TOK) // BLOCK
-        part = lax.broadcasted_iota(jnp.int32, (2 * TOK, 1), 0) // BLOCK
-        for g, q_ref, out_ref in ((1, other_ref, out_other), (0, mine_ref, out_mine)):
-            yq = 1 if far else y
-            cq = c if g == 0 else 1 - c
-            first = (yq * 16 + z * 2 + cq) * 4
-            low = jnp.zeros((2 * TOK, 1), jnp.int32)
-            high = jnp.zeros((2 * TOK, 1), jnp.int32)
-            for p in range(8):
-                copy, block = p // 4, first + p % 4
-                low = jnp.where(part == p, table_ref[copy, block], low)
-                high = jnp.where(part == p, block - copy, high)
-            visible = (key_block >= low) & (key_block <= high)
-            lses = []
-            for h in range(2):
-                q = q_ref[:, head(h)]
-                scores = lax.dot_general(
-                    q, keys[:, head(h)], (((1,), (1,)), ((), ())), preferred_element_type=jnp.float32
-                ) * SCALE2
-                scores = jnp.where(visible, scores, HIDDEN)
-                peak = jnp.maximum(jnp.max(scores, axis=-1, keepdims=True), FLOOR)
-                near_part = g == 0 and not far
-                if near_part:
-                    own = lax.dot_general(
-                        q[TOK:], kvn_ref[:, head(h)], (((1,), (1,)), ((), ())),
-                        preferred_element_type=jnp.float32,
-                    ) * SCALE2
-                    near = (
-                        lax.broadcasted_iota(jnp.int32, (TOK, TOK), 0) // BLOCK
-                        == lax.broadcasted_iota(jnp.int32, (TOK, TOK), 1) // BLOCK
-                    )
-                    own = jnp.where(near, own, HIDDEN)
-                    peak_own = jnp.maximum(peak[TOK:], jnp.max(own, axis=-1, keepdims=True))
-                    peak = jnp.concatenate([peak[:TOK], peak_own], axis=0)
-                weights = jnp.exp2(scores - peak)
-                total = jnp.sum(weights, axis=-1, keepdims=True)
-                weighted = jnp.dot(
-                    weights.astype(jnp.bfloat16), keys[:, head(2 + h)], preferred_element_type=jnp.float32
-                )
-                if near_part:
-                    wown = jnp.exp2(own - peak_own)
-                    total = total + jnp.concatenate(
-                        [jnp.zeros((TOK, 1), jnp.float32), jnp.sum(wown, axis=-1, keepdims=True)], axis=0
-                    )
-                    extra = jnp.dot(
-                        wown.astype(jnp.bfloat16), kvn_ref[:, head(2 + h)], preferred_element_type=jnp.float32
-                    )
-                    weighted = weighted + jnp.concatenate(
-                        [jnp.zeros((TOK, HEAD_DIM), jnp.float32), extra], axis=0
-                    )
-                some = total > 0.0
-                safe = jnp.where(some, total, 1.0)
-                out_ref[:, head(h)] = (weighted / safe).astype(jnp.bfloat16)
-                lses.append(jnp.where(some, peak + jnp.log2(safe), FLOOR))
-            out_ref[:, 256:] = pack_stats(lses)
-
-    if far:
+        keys[: 2 * TOK] = three_ref[...].reshape(2 * TOK, 512)
+        keys[2 * TOK :] = half_ref[...]
+        tiles = LATE
+        if line == 1:
+            mine = jnp.where(y == 1, q_ref[...], far_ref[...])
+            other = jnp.where(y == 1, other_ref[...], far_other_ref[...])
+        else:
+            mine, other = q_ref[...], other_ref[...]
+        pack(merge(saved(swap_ref), partial(other, keys, tiles, table_ref, line, 1 - c)), out_other)
+        pack(merge(saved(mine_ref), partial(mine, keys, tiles, table_ref, line, c)), out_mine)
+
+    if line == 1:
+        work()
+    else:
         pl.when(y == 0)(work)
 
         @pl.when(y == 1)
         def _():
             out_mine[...] = jnp.zeros_like(out_mine)
             out_other[...] = jnp.zeros_like(out_other)
-    else:
-        work()
-
-
-def attend(table, mine, other, key_values, *extra):
-    far = not extra
-
+
+
+def late(line, table, q, other, far, far_other, three, half, mine, swapped, after):
     def kernel(*refs):
-        attend_kernel(far, *refs)
+        late_kernel(line, *refs)
 
     return pl.pallas_call(
         kernel,
         out_shape=(struct(2 * TOK, 384), struct(2 * TOK, 384)),
-        in_specs=[SMEM] + [VMEM] * (2 + NZ) + ([] if far else [VMEM, ANY]),
+        in_specs=[SMEM] + [VMEM] * 8 + [ANY],
         out_specs=(VMEM, VMEM),
-        scratch_shapes=[pltpu.VMEM((NZ * TOK, 512), jnp.bfloat16)],
+        scratch_shapes=[pltpu.VMEM((len(LATE) * TOK, 512), jnp.bfloat16)],
         compiler_params=params(),
         cost_estimate=cost(4, 1 << 29),
-        name="attend_far" if far else "attend_near",
-    )(table, mine, other, *key_values, *extra)
-
-
-def merge(a, b):
-    outs, lses = [], []
-    sa, sb = unpack_stats(a[:, 256:]), unpack_stats(b[:, 256:])
-    for h in range(2):
-        peak = jnp.maximum(sa[h], sb[h])
-        wa, wb = jnp.exp2(sa[h] - peak), jnp.exp2(sb[h] - peak)
-        total = wa + wb
-        mixed = a[:, head(h)].astype(jnp.float32) * wa + b[:, head(h)].astype(jnp.float32) * wb
-        outs.append(mixed / total)
-        lses.append(peak + jnp.log2(total))
-    return outs, lses
+        name="late_upper" if line == 1 else "late_lower",
+    )(table, q, other, far, far_other, three, half, mine, swapped, after)
 
 
 def merge_kernel(mine_ref, swap_ref, out_ref):
-    outs, lses = merge(mine_ref[...], swap_ref[...])
-    for h in range(2):
-        out_ref[:, head(h)] = outs[h].astype(jnp.bfloat16)
-    out_ref[:, 256:] = pack_stats(lses)
+    pack(merge(unpack(mine_ref), unpack(swap_ref)), out_ref)
 
 
 def merge_cores(mine, swapped):
@@ -337,16 +406,17 @@
         out_specs=VMEM,
         compiler_params=params(),
         cost_estimate=cost(1),
+        name="merge",
     )(mine, swapped)
 
 
-def output_kernel(self_ref, far_ref, w_ref, *refs):
+def output_kernel(upper_ref, lower_ref, far_ref, w_ref, *refs):
     att = refs[-1]
-    outs, _ = merge(self_ref[...], far_ref[...])
+    outs, _ = merge(unpack(upper_ref), unpack(far_ref))
     upper_line = place()[0] == 1
+    lower, _ = unpack(lower_ref)
     for h in range(2):
-        alone = self_ref[:, head(h)].astype(jnp.float32)
-        value = jnp.where(upper_line, outs[h], alone).astype(jnp.bfloat16)
+        value = jnp.where(upper_line, outs[h], lower[h]).astype(jnp.bfloat16)
         for t in range(NT):
             for s in range(2):
                 att[t, s * 16 : (s + 1) * 16, head(h)] = value[s * TOK + t * 16 : s * TOK + (t + 1) * 16]
@@ -365,18 +435,18 @@
             refs[0][:, :, cols] = terms.reshape(NT, 32, 512)
 
 
-def output(mine, far, w_out):
+def output(upper, lower, far, w_out):
     shapes = (struct(32, D),) * NT if TERMS_PP else (struct(NT, 32, D),)
     return pl.pallas_call(
         output_kernel,
         out_shape=shapes,
-        in_specs=[VMEM, VMEM, VMEM],
+        in_specs=[VMEM] * 4,
         out_specs=(VMEM,) * len(shapes),
         scratch_shapes=[pltpu.VMEM((NT, 32, 256), jnp.bfloat16)],
         compiler_params=params(),
         cost_estimate=cost(4, 1 << 29),
         name="terms",
-    )(mine, far, w_out)
+    )(upper, lower, far, w_out)
 
 
 def sum_kernel(*refs):
@@ -391,19 +461,14 @@
 
 
 def sum_terms(blocks):
-    tile = 1024
-    if TERMS_PP:
-        specs = [pl.BlockSpec((32, tile), lambda i: (0, i))] * NT
-    else:
-        specs = [pl.BlockSpec((NT, 32, tile), lambda i: (0, 0, i))]
     return pl.pallas_call(
         sum_kernel,
-        grid=(D // tile,),
         out_shape=(struct(16, D), struct(16, D)),
-        in_specs=specs,
-        out_specs=(pl.BlockSpec((16, tile), lambda i: (0, i)),) * 2,
+        in_specs=[VMEM] * len(blocks),
+        out_specs=(VMEM, VMEM),
         compiler_params=params(),
         cost_estimate=cost(2),
+        name="sum_terms",
     )(*blocks)
 
 
@@ -457,20 +522,25 @@
     w, masked = load_weights(mask_row, wq, wk, wv)
     kv, kvn, all_rows = project_keys(gathered, w, masked, cosine, sine)
 
-    pieces = [kv]
-    for s in range(1, NZ):
-        pieces.append(ctx_move(kv, lambda y, z, c: (y, (z + s) % NZ, c)))
+    def along(step):
+        return lambda y, z, c: (y, (z + (NZ - step if c else step)) % NZ, c)
+
+    pair = jnp.stack([kv, swap(kv)])
+    two = ctx_move(pair, along(2))
+    one = ctx_move(pair, along(1))
+    three = ctx_move(two, along(1))
+    half = ctx_move(two[0], along(2))
     q = project_queries(all_rows, w, masked, cosine, sine)
-    q_far = ctx_move(q, lambda y, z, c: (0, z, c) if y == 1 else None)
-    q_other = swap(q)
-    q_far_other = swap(q_far)
-
-    far, far_other = attend(table, q_far, q_far_other, pieces)
-    far = merge_cores(far, swap(far_other))
-    returned = ctx_move(far, lambda y, z, c: (1, z, c) if y == 0 else None)
-    mine, other = attend(table, q, q_other, pieces, kvn, far)
-    mine = merge_cores(mine, swap(other))
-    terms = list(output(mine, returned, w_out))
+    far = ctx_move(q, lambda y, z, c: (0, z, c) if y == 1 else None)
+    queries = (q, swap(q), far, swap(far))
+
+    up_mine, up_other, low_mine, low_other = early(table, *queries, pair, two, one, kvn)
+    mine, other = late(1, table, *queries, three, half, up_mine, up_other, kvn)
+    upper = merge_cores(mine, swap(other))
+    returned = ctx_move(upper, lambda y, z, c: (1, z, c) if y == 0 else None)
+    mine, other = late(0, table, *queries, three, half, low_mine, low_other, upper)
+    lower = merge_cores(mine, swap(other))
+    terms = list(output(upper, lower, returned, w_out))
     if TERMS_PP:
         for r in range(1, NT):
             terms[r] = tp_move(terms[r], r)

time: 109 us -> 97.6 us (0.90)
  the two profiles are of different devices: /device:TPU:32 before, /device:TPU:28 now
where the time goes in v2:
time: 97.6 us; the launch traced here: 97.5 us
  starting transfers between devices  46.5 us (48%)
  waiting for transfers between devices  34.4 us (35%)
  Pallas kernels  15.1 us (15%)
    ppermute x14, starting transfers between devices, tp_move(): return lax.ppermute(x, 'tp', [(i, relative(i, r)) for i in range(NT)])  31.2 us
    ppermute x14, waiting for transfers between devices, tp_move(): return lax.ppermute(x, 'tp', [(i, relative(i, r)) for i in range(NT)])  18 us
    ppermute x11, waiting for transfers between devices, ctx_move(): return lax.ppermute(x, 'ctx', ctx_perm(move))  16.4 us
    ppermute x11, starting transfers between devices, ctx_move(): return lax.ppermute(x, 'ctx', ctx_perm(move))  15.4 us
    pallas_call x1, Pallas kernels, load_weights(): pl.pallas_call(weights_kernel, out_shape=(struct(D, 768), struct(8, 768,...  3.81 us
    pallas_call x2, Pallas kernels, late(): pl.pallas_call(kernel, out_shape=(struct(2 * TOK, 384), struct(2 * TOK, 3...  2.97 us
    pallas_call x1, Pallas kernels, early(): pl.pallas_call(early_kernel, out_shape=(struct(2 * TOK, 512, dtype=jnp.fl...  2.72 us
  transfers between devices with their start and end apart: 25, of which 11 were waited for; matrix products, arithmetic and copies ran while one was open for 1% of the time, Pallas kernels for 8%

profile of v2, /device:TPU:28, one launch (start us, length us, event | category | flops | bytes accessed | tf_op | source)
XLA Modules:
  0.0 97.5 jit_solution(1043469401090828303)
XLA Ops:
  0.6 1.1 %norm.1 = (bf16[16,4224]{1,0:T(8,128)(2,1)S(1)}, bf16[16,4096]{1,0:T(8,128)(2,1)S(1)}) custom-call(bf16[16,4096]{1,0:T(8,128)(2,1)} %tok_hbm.1, s32[16]{0:T(128)} %flag_hbm.1, bf16[32,128]{1,0:T(8,128)(2,1)} %bitcast.12, bf16[32,128]{1,0:T(8,128)(2,1)} %bitcast.13), custom_call_target="tpu_custom_call" | custom-call | flops 1048576 | bytes 1048576 | tf_op jit(solution)/shard_map/norm/pallas_call | solution.py:80
  1.7 1.3 %collective-permute-start.3 = (bf16[16,4224]{1,0:T(8,128)(2,1)S(1)}, bf16[16,4224]{1,0:T(8,128)(2,1)S(1)}, u32[]{:S(2)}, u32[]{:S(2)}) collective-permute-start(bf16[16,4224]{1,0:T(8,128)(2,1)S(1)} %get-tuple-element.25.refs_0_), channel_id=1, source_target_pairs={{0,4},{1,5},{2,6},{3,7},{4,0},{5,1},{6,2},{7,3},{8,12},{9,13},{10,... | collective-permute-start | bytes 405512 | tf_op jit(solution)/shard_map/ppermute | solution.py:496
  3.6 2.7 %collective-permute-start.1 = (bf16[16,4224]{1,0:T(8,128)(2,1)S(1)}, bf16[16,4224]{1,0:T(8,128)(2,1)S(1)}, u32[]{:S(2)}, u32[]{:S(2)}) collective-permute-start(bf16[16,4224]{1,0:T(8,128)(2,1)S(1)} %get-tuple-element.25.refs_0_), channel_id=1, source_target_pairs={{0,2},{1,3},{2,0},{3,1},{4,6},{5,7},{6,4},{7,5},{8,10},{9,11},{10,... | collective-permute-start | bytes 405512 | tf_op jit(solution)/shard_map/ppermute | solution.py:496
  6.4 2.3 %collective-permute-done.3.refs_4_ = bf16[16,4224]{1,0:T(8,128)(2,1)S(1)} collective-permute-done((bf16[16,4224]{1,0:T(8,128)(2,1)S(1)}, bf16[16,4224]{1,0:T(8,128)(2,1)S(1)}, u32[]{:S(2)}, u32[]{:S(2)}) %collective-permute-start.3) | collective-permute-done | bytes 135200 | tf_op jit(solution)/shard_map/ppermute | solution.py:496
  9.2 2.7 %collective-permute-start.5 = (bf16[16,4224]{1,0:T(8,128)(2,1)S(1)}, bf16[16,4224]{1,0:T(8,128)(2,1)S(1)}, u32[]{:S(2)}, u32[]{:S(2)}) collective-permute-start(bf16[16,4224]{1,0:T(8,128)(2,1)S(1)} %collective-permute-done.3.refs_4_), channel_id=1, source_target_pairs={{0,2},{1,3},{2,0},{3,1},{4,6},{5,7},{6,4},{7,5},{8,10},{9,11},{10,... | collective-permute-start | bytes 405512 | tf_op jit(solution)/shard_map/ppermute | solution.py:496
  11.9 2.2 %collective-permute-start.6 = (bf16[16,4224]{1,0:T(8,128)(2,1)S(1)}, bf16[16,4224]{1,0:T(8,128)(2,1)S(1)}, u32[]{:S(2)}, u32[]{:S(2)}) collective-permute-start(bf16[16,4224]{1,0:T(8,128)(2,1)S(1)} %collective-permute-done.3.refs_4_), channel_id=1, source_target_pairs={{0,1},{1,2},{2,3},{3,0},{4,5},{5,6},{6,7},{7,4},{8,9},{9,10},{10,1... | collective-permute-start | bytes 405512 | tf_op jit(solution)/shard_map/ppermute | solution.py:496
  14.5 3.8 %weights.1 = (bf16[4096,768]{1,0:T(8,128)(2,1)S(1)}, f32[8,768]{1,0:T(8,128)S(1)}) custom-call(bf16[16,4096]{1,0:T(8,128)(2,1)S(1)} %get-tuple-element.26.mask_ref, bf16[4096,256]{1,0:T(8,128)(2,1)} %wq_hbm.1, bf16[4096,256]{1,0:T(8,128)(2,1)} %wk_hbm.1, bf16[4096,256]{1,0:T(8,128)(2,1)} %wv_hbm.1), custom_call_target="tpu_custom_call" | custom-call | flops 1048576 | bytes 12582912 | tf_op jit(solution)/shard_map/weights/pallas_call | solution.py:119
  18.6 0.9 keys.1
  19.7 1.2 %collective-permute-done.10 = bf16[128,512]{1,0:T(8,128)(2,1)S(1)} collective-permute-done((bf16[128,512]{1,0:T(8,128)(2,1)S(1)}, bf16[128,512]{1,0:T(8,128)(2,1)S(1)}, u32[]{:S(2)}, u32[]{:S(2)}) %collective-permute-start.10) | collective-permute-done | bytes 131104 | tf_op jit(solution)/shard_map/ppermute | solution.py:488
  20.9 3.3 %collective-permute-start.11 = (bf16[2,128,512]{2,1,0:T(8,128)(2,1)S(1)}, bf16[2,128,512]{2,1,0:T(8,128)(2,1)S(1)}, u32[]{:S(2)}, u32[]{:S(2)}) collective-permute-start(bf16[2,128,512]{2,1,0:T(8,128)(2,1)S(1)} %pad_maximum_fusion.own_ref), channel_id=1, source_target_pairs={{0,32},{8,104},{16,48},{24,120},{32,64},{40,8},{48,80},{56,24},{64... | collective-permute-start | bytes 786440 | tf_op jit(solution)/shard_map/ppermute | solution.py:488
  24.8 1.9 %collective-permute-start.8 = (bf16[256,256]{1,0:T(8,128)(2,1)S(1)}, bf16[256,256]{1,0:T(8,128)(2,1)S(1)}, u32[]{:S(2)}, u32[]{:S(2)}) collective-permute-start(bf16[256,256]{1,0:T(8,128)(2,1)S(1)} %queries.1.q_ref.refs_1_), channel_id=1, source_target_pairs={{128,0},{136,8},{144,16},{152,24},{160,32},{168,40},{176,48},{184,... | collective-permute-start | bytes 393224 | tf_op jit(solution)/shard_map/ppermute | solution.py:488
  26.7 2.7 %collective-permute-start.7 = (bf16[256,256]{1,0:T(8,128)(2,1)S(1)}, bf16[256,256]{1,0:T(8,128)(2,1)S(1)}, u32[]{:S(2)}, u32[]{:S(2)}) collective-permute-start(bf16[256,256]{1,0:T(8,128)(2,1)S(1)} %queries.1.q_ref.refs_1_), channel_id=1, source_target_pairs={{0,8},{8,0},{16,24},{24,16},{32,40},{40,32},{48,56},{56,48},{64,72... | collective-permute-start | bytes 393224 | tf_op jit(solution)/shard_map/ppermute | solution.py:488
  29.4 1.0 %collective-permute-start.14 = (bf16[2,128,512]{2,1,0:T(8,128)(2,1)S(1)}, bf16[2,128,512]{2,1,0:T(8,128)(2,1)S(1)}, u32[]{:S(2)}, u32[]{:S(2)}) collective-permute-start(bf16[2,128,512]{2,1,0:T(8,128)(2,1)S(1)} %pad_maximum_fusion.own_ref), channel_id=1, source_target_pairs={{0,16},{8,120},{16,32},{24,8},{32,48},{40,24},{48,64},{56,40},{64,... | collective-permute-start | bytes 786440 | tf_op jit(solution)/shard_map/ppermute | solution.py:488
  30.4 0.8 collective-permute-start.9
  31.3 1.0 %collective-permute-done.11.two_ref = bf16[2,128,512]{2,1,0:T(8,128)(2,1)S(1)} collective-permute-done((bf16[2,128,512]{2,1,0:T(8,128)(2,1)S(1)}, bf16[2,128,512]{2,1,0:T(8,128)(2,1)S(1)}, u32[]{:S(2)}, u32[]{:S(2)}) %collective-permute-start.11) | collective-permute-done | bytes 262176 | tf_op jit(solution)/shard_map/ppermute | solution.py:488
  32.2 3.3 %collective-permute-start.12 = (bf16[2,128,512]{2,1,0:T(8,128)(2,1)S(1)}, bf16[2,128,512]{2,1,0:T(8,128)(2,1)S(1)}, u32[]{:S(2)}, u32[]{:S(2)}) collective-permute-start(bf16[2,128,512]{2,1,0:T(8,128)(2,1)S(1)} %collective-permute-done.11.two_ref), channel_id=1, source_target_pairs={{0,16},{8,120},{16,32},{24,8},{32,48},{40,24},{48,64},{56,40},{64,... | collective-permute-start | bytes 786440 | tf_op jit(solution)/shard_map/ppermute | solution.py:488
  37.0 2.7 %early.1 = (f32[256,512]{1,0:T(8,128)S(1)}, f32[256,512]{1,0:T(8,128)S(1)}, f32[256,512]{1,0:T(8,128)S(1)}, f32[256,512]{1,0:T(8,128)S(1)}) custom-call(s32[2,128]{1,0:T(2,128)S(1)} %pad_add_fusion.table_ref.refs_0_, bf16[256,256]{1,0:T(8,128)(2,1)S(1)} %queries.1.q_ref.refs_1_, bf16[256,256]{1,0:T(8,128)(2,1)S(1)} %collective-permute-done.7.other_ref.refs_2_, ...), custom_call_target="tpu_custom_call" | custom-call | flops 536870912 | bytes 4194304 | tf_op jit(solution)/shard_map/early/pallas_call | solution.py:342
  39.7 4.7 %collective-permute-done.13.refs_6_ = bf16[128,512]{1,0:T(8,128)(2,1)S(1)} collective-permute-done((bf16[128,512]{1,0:T(8,128)(2,1)S(1)}, bf16[128,512]{1,0:T(8,128)(2,1)S(1)}, u32[]{:S(2)}, u32[]{:S(2)}) %collective-permute-start.13) | collective-permute-done | bytes 131104 | tf_op jit(solution)/shard_map/ppermute | solution.py:488
  44.4 2.4 %late_upper.1 = (bf16[256,384]{1,0:T(8,128)(2,1)S(1)}, bf16[256,384]{1,0:T(8,128)(2,1)S(1)}) custom-call(s32[2,128]{1,0:T(2,128)S(1)} %pad_add_fusion.table_ref.refs_0_, bf16[256,256]{1,0:T(8,128)(2,1)S(1)} %queries.1.q_ref.refs_1_, bf16[256,256]{1,0:T(8,128)(2,1)S(1)} %collective-permute-done.7.other_ref.refs_2_, ...), custom_call_target="tpu_custom_call" | custom-call | flops 536870912 | bytes 4194304 | tf_op jit(solution)/shard_map/late_upper/pallas_call | solution.py:385
  46.9 1.4 %collective-permute-done.15.swap_ref = bf16[256,384]{1,0:T(8,128)(2,1)S(1)} collective-permute-done((bf16[256,384]{1,0:T(8,128)(2,1)S(1)}, bf16[256,384]{1,0:T(8,128)(2,1)S(1)}, u32[]{:S(2)}, u32[]{:S(2)}) %collective-permute-start.15) | collective-permute-done | bytes 196640 | tf_op jit(solution)/shard_map/ppermute | solution.py:488
  49.7 1.3 %collective-permute-start.17 = (bf16[256,384]{1,0:T(8,128)(2,1)S(1)}, bf16[256,384]{1,0:T(8,128)(2,1)S(1)}, u32[]{:S(2)}, u32[]{:S(2)}) collective-permute-start(bf16[256,384]{1,0:T(8,128)(2,1)S(1)} %merge.2.refs_9_.upper_ref), channel_id=1, source_target_pairs={{0,128},{8,136},{16,144},{24,152},{32,160},{40,168},{48,176},{56,1... | collective-permute-start | bytes 589832 | tf_op jit(solution)/shard_map/ppermute | solution.py:488
  51.5 7.2 %collective-permute-done.17.far_ref = bf16[256,384]{1,0:T(8,128)(2,1)S(1)} collective-permute-done((bf16[256,384]{1,0:T(8,128)(2,1)S(1)}, bf16[256,384]{1,0:T(8,128)(2,1)S(1)}, u32[]{:S(2)}, u32[]{:S(2)}) %collective-permute-start.17) | collective-permute-done | bytes 196640 | tf_op jit(solution)/shard_map/ppermute | solution.py:488
  58.8 1.1 %terms.1 = (bf16[32,4096]{1,0:T(8,128)(2,1)S(1)}, bf16[32,4096]{1,0:T(8,128)(2,1)S(1)}, bf16[32,4096]{1,0:T(8,128)(2,1)S(1)}, bf16[32,4096]{1,0:T(8,128)(2,1)S(1...) custom-call(bf16[256,384]{1,0:T(8,128)(2,1)S(1)} %merge.2.refs_9_.up, ...), custom_call_target="tpu_custom_call" | custom-call | flops 536870912 | bytes 4194304 | tf_op jit(solution)/shard_map/terms/pallas_call | solution.py:440
  59.9 1.3 %collective-permute-start.18 = (bf16[32,4096]{1,0:T(8,128)(2,1)S(1)}, bf16[32,4096]{1,0:T(8,128)(2,1)S(1)}, u32[]{:S(2)}, u32[]{:S(2)}) collective-permute-start(bf16[32,4096]{1,0:T(8,128)(2,1)S(1)} %get-tuple-element.41), channel_id=1, source_target_pairs={{0,1},{1,2},{2,3},{3,0},{4,5},{5,6},{6,7},{7,4},{8,9},{9,10},{10,1... | collective-permute-start | bytes 786440 | tf_op jit(solution)/shard_map/ppermute | solution.py:496
  61.2 1.6 %collective-permute-start.19 = (bf16[32,4096]{1,0:T(8,128)(2,1)S(1)}, bf16[32,4096]{1,0:T(8,128)(2,1)S(1)}, u32[]{:S(2)}, u32[]{:S(2)}) collective-permute-start(bf16[32,4096]{1,0:T(8,128)(2,1)S(1)} %get-tuple-element.42), channel_id=1, source_target_pairs={{0,2},{1,3},{2,0},{3,1},{4,6},{5,7},{6,4},{7,5},{8,10},{9,11},{10,... | collective-permute-start | bytes 786440 | tf_op jit(solution)/shard_map/ppermute | solution.py:496
  62.8 2.5 %collective-permute-start.20 = (bf16[32,4096]{1,0:T(8,128)(2,1)S(1)}, bf16[32,4096]{1,0:T(8,128)(2,1)S(1)}, u32[]{:S(2)}, u32[]{:S(2)}) collective-permute-start(bf16[32,4096]{1,0:T(8,128)(2,1)S(1)} %get-tuple-element.43), channel_id=1, source_target_pairs={{0,3},{1,0},{2,1},{3,2},{4,7},{5,4},{6,5},{7,6},{8,11},{9,8},{10,9... | collective-permute-start | bytes 786440 | tf_op jit(solution)/shard_map/ppermute | solution.py:496
  65.3 3.1 %collective-permute-start.21 = (bf16[32,4096]{1,0:T(8,128)(2,1)S(1)}, bf16[32,4096]{1,0:T(8,128)(2,1)S(1)}, u32[]{:S(2)}, u32[]{:S(2)}) collective-permute-start(bf16[32,4096]{1,0:T(8,128)(2,1)S(1)} %get-tuple-element.44), channel_id=1, source_target_pairs={{0,4},{1,5},{2,6},{3,7},{4,0},{5,1},{6,2},{7,3},{8,12},{9,13},{10,... | collective-permute-start | bytes 786440 | tf_op jit(solution)/shard_map/ppermute | solution.py:496
  68.4 12.6 %collective-permute-start.23 = (bf16[32,4096]{1,0:T(8,128)(2,1)S(1)}, bf16[32,4096]{1,0:T(8,128)(2,1)S(1)}, u32[]{:S(2)}, u32[]{:S(2)}) collective-permute-start(bf16[32,4096]{1,0:T(8,128)(2,1)S(1)} %get-tuple-element.46), channel_id=1, source_target_pairs={{0,6},{1,7},{2,4},{3,5},{4,2},{5,3},{6,0},{7,1},{8,14},{9,15},{10,... | collective-permute-start | bytes 786440 | tf_op jit(solution)/shard_map/ppermute | solution.py:496
  81.0 1.5 %collective-permute-done.22.refs_5_ = bf16[32,4096]{1,0:T(8,128)(2,1)S(1)} collective-permute-done((bf16[32,4096]{1,0:T(8,128)(2,1)S(1)}, bf16[32,4096]{1,0:T(8,128)(2,1)S(1)}, u32[]{:S(2)}, u32[]{:S(2)}) %collective-permute-start.22) | collective-permute-done | bytes 262176 | tf_op jit(solution)/shard_map/ppermute | solution.py:496
  82.6 12.9 %collective-permute-done.23.refs_6_ = bf16[32,4096]{1,0:T(8,128)(2,1)S(1)} collective-permute-done((bf16[32,4096]{1,0:T(8,128)(2,1)S(1)}, bf16[32,4096]{1,0:T(8,128)(2,1)S(1)}, u32[]{:S(2)}, u32[]{:S(2)}) %collective-permute-start.23) | collective-permute-done | bytes 262176 | tf_op jit(solution)/shard_map/ppermute | solution.py:496
  95.5 1.1 %collective-permute-done.24.refs_7_ = bf16[32,4096]{1,0:T(8,128)(2,1)S(1)} collective-permute-done((bf16[32,4096]{1,0:T(8,128)(2,1)S(1)}, bf16[32,4096]{1,0:T(8,128)(2,1)S(1)}, u32[]{:S(2)}, u32[]{:S(2)}) %collective-permute-start.24) | collective-permute-done | bytes 262176 | tf_op jit(solution)/shard_map/ppermute | solution.py:496
  96.6 0.9 sum_terms.1
  (42 shorter events, 5.9 us)
Async XLA Ops:
  1.7 6.9 %collective-permute-start.3 = (bf16[16,4224]{1,0:T(8,128)(2,1)S(1)}, bf16[16,4224]{1,0:T(8,128)(2,1)S(1)}, u32[]{:S(2)}, u32[]{:S(2)}) collective-permute-start(bf16[16,4224]{1,0:T(8,128)(2,1)S(1)} %get-tuple-element.25.refs_0_), channel_id=1, source_target_pairs={{0,4},{1,5},{2,6},{3,7},{4,0},{5,1},{6,2},{7,3},{8,12},{9,13},{10,... | collective-permute-start | bytes 405512 | tf_op jit(solution)/shard_map/ppermute | solution.py:496
  3.1 8.9 %collective-permute-start = (bf16[16,4224]{1,0:T(8,128)(2,1)S(1)}, bf16[16,4224]{1,0:T(8,128)(2,1)S(1)}, u32[]{:S(2)}, u32[]{:S(2)}) collective-permute-start(bf16[16,4224]{1,0:T(8,128)(2,1)S(1)} %get-tuple-element.25.refs_0_), channel_id=1, source_target_pairs={{0,3},{1,0},{2,1},{3,2},{4,7},{5,4},{6,5},{7,6},{8,11},{9,8},{10,9... | collective-permute-start | bytes 405512 | tf_op jit(solution)/shard_map/ppermute | solution.py:496
  3.6 14.8 %collective-permute-start.1 = (bf16[16,4224]{1,0:T(8,128)(2,1)S(1)}, bf16[16,4224]{1,0:T(8,128)(2,1)S(1)}, u32[]{:S(2)}, u32[]{:S(2)}) collective-permute-start(bf16[16,4224]{1,0:T(8,128)(2,1)S(1)} %get-tuple-element.25.refs_0_), channel_id=1, source_target_pairs={{0,2},{1,3},{2,0},{3,1},{4,6},{5,7},{6,4},{7,5},{8,10},{9,11},{10,... | collective-permute-start | bytes 405512 | tf_op jit(solution)/shard_map/ppermute | solution.py:496
  6.3 12.1 %collective-permute-start.2 = (bf16[16,4224]{1,0:T(8,128)(2,1)S(1)}, bf16[16,4224]{1,0:T(8,128)(2,1)S(1)}, u32[]{:S(2)}, u32[]{:S(2)}) collective-permute-start(bf16[16,4224]{1,0:T(8,128)(2,1)S(1)} %get-tuple-element.25.refs_0_), channel_id=1, source_target_pairs={{0,1},{1,2},{2,3},{3,0},{4,5},{5,6},{6,7},{7,4},{8,9},{9,10},{10,1... | collective-permute-start | bytes 405512 | tf_op jit(solution)/shard_map/ppermute | solution.py:496
  8.7 9.7 %collective-permute-start.4 = (bf16[16,4224]{1,0:T(8,128)(2,1)S(1)}, bf16[16,4224]{1,0:T(8,128)(2,1)S(1)}, u32[]{:S(2)}, u32[]{:S(2)}) collective-permute-start(bf16[16,4224]{1,0:T(8,128)(2,1)S(1)} %collective-permute-done.3.refs_4_), channel_id=1, source_target_pairs={{0,3},{1,0},{2,1},{3,2},{4,7},{5,4},{6,5},{7,6},{8,11},{9,8},{10,9... | collective-permute-start | bytes 405512 | tf_op jit(solution)/shard_map/ppermute | solution.py:496
  9.2 9.2 %collective-permute-start.5 = (bf16[16,4224]{1,0:T(8,128)(2,1)S(1)}, bf16[16,4224]{1,0:T(8,128)(2,1)S(1)}, u32[]{:S(2)}, u32[]{:S(2)}) collective-permute-start(bf16[16,4224]{1,0:T(8,128)(2,1)S(1)} %collective-permute-done.3.refs_4_), channel_id=1, source_target_pairs={{0,2},{1,3},{2,0},{3,1},{4,6},{5,7},{6,4},{7,5},{8,10},{9,11},{10,... | collective-permute-start | bytes 405512 | tf_op jit(solution)/shard_map/ppermute | solution.py:496
  11.9 6.6 %collective-permute-start.6 = (bf16[16,4224]{1,0:T(8,128)(2,1)S(1)}, bf16[16,4224]{1,0:T(8,128)(2,1)S(1)}, u32[]{:S(2)}, u32[]{:S(2)}) collective-permute-start(bf16[16,4224]{1,0:T(8,128)(2,1)S(1)} %collective-permute-done.3.refs_4_), channel_id=1, source_target_pairs={{0,1},{1,2},{2,3},{3,0},{4,5},{5,6},{6,7},{7,4},{8,9},{9,10},{10,1... | collective-permute-start | bytes 405512 | tf_op jit(solution)/shard_map/ppermute | solution.py:496
  18.6 1.0 %copy-start.1 = (s32[128,128]{1,0:T(8,128)S(1)}, s32[128,128]{1,0:T(8,128)}, u32[]{:S(2)}) copy-start(s32[128,128]{1,0:T(8,128)} %param.17) | copy-start | bytes 196612
  19.5 1.4 %collective-permute-start.10 = (bf16[128,512]{1,0:T(8,128)(2,1)S(1)}, bf16[128,512]{1,0:T(8,128)(2,1)S(1)}, u32[]{:S(2)}, u32[]{:S(2)}) collective-permute-start(bf16[128,512]{1,0:T(8,128)(2,1)S(1)} %get-tuple-element.30), channel_id=1, source_target_pairs={{0,8},{8,0},{16,24},{24,16},{32,40},{40,32},{48,56},{56,48},{64,72... | collective-permute-start | bytes 393224 | tf_op jit(solution)/shard_map/ppermute | solution.py:488
  20.9 11.3 %collective-permute-start.11 = (bf16[2,128,512]{2,1,0:T(8,128)(2,1)S(1)}, bf16[2,128,512]{2,1,0:T(8,128)(2,1)S(1)}, u32[]{:S(2)}, u32[]{:S(2)}) collective-permute-start(bf16[2,128,512]{2,1,0:T(8,128)(2,1)S(1)} %pad_maximum_fusion.own_ref), channel_id=1, source_target_pairs={{0,32},{8,104},{16,48},{24,120},{32,64},{40,8},{48,80},{56,24},{64... | collective-permute-start | bytes 786440 | tf_op jit(solution)/shard_map/ppermute | solution.py:488
  24.8 5.6 %collective-permute-start.8 = (bf16[256,256]{1,0:T(8,128)(2,1)S(1)}, bf16[256,256]{1,0:T(8,128)(2,1)S(1)}, u32[]{:S(2)}, u32[]{:S(2)}) collective-permute-start(bf16[256,256]{1,0:T(8,128)(2,1)S(1)} %queries.1.q_ref.refs_1_), channel_id=1, source_target_pairs={{128,0},{136,8},{144,16},{152,24},{160,32},{168,40},{176,48},{184,... | collective-permute-start | bytes 393224 | tf_op jit(solution)/shard_map/ppermute | solution.py:488
  26.7 9.5 %collective-permute-start.7 = (bf16[256,256]{1,0:T(8,128)(2,1)S(1)}, bf16[256,256]{1,0:T(8,128)(2,1)S(1)}, u32[]{:S(2)}, u32[]{:S(2)}) collective-permute-start(bf16[256,256]{1,0:T(8,128)(2,1)S(1)} %queries.1.q_ref.refs_1_), channel_id=1, source_target_pairs={{0,8},{8,0},{16,24},{24,16},{32,40},{40,32},{48,56},{56,48},{64,72... | collective-permute-start | bytes 393224 | tf_op jit(solution)/shard_map/ppermute | solution.py:488
  29.4 7.6 %collective-permute-start.14 = (bf16[2,128,512]{2,1,0:T(8,128)(2,1)S(1)}, bf16[2,128,512]{2,1,0:T(8,128)(2,1)S(1)}, u32[]{:S(2)}, u32[]{:S(2)}) collective-permute-start(bf16[2,128,512]{2,1,0:T(8,128)(2,1)S(1)} %pad_maximum_fusion.own_ref), channel_id=1, source_target_pairs={{0,16},{8,120},{16,32},{24,8},{32,48},{40,24},{48,64},{56,40},{64,... | collective-permute-start | bytes 786440 | tf_op jit(solution)/shard_map/ppermute | solution.py:488
  30.4 5.8 %collective-permute-start.9 = (bf16[256,256]{1,0:T(8,128)(2,1)S(1)}, bf16[256,256]{1,0:T(8,128)(2,1)S(1)}, u32[]{:S(2)}, u32[]{:S(2)}) collective-permute-start(bf16[256,256]{1,0:T(8,128)(2,1)S(1)} %collective-permute-done.8.far_ref.refs_3_), channel_id=1, source_target_pairs={{0,8},{8,0},{16,24},{24,16},{32,40},{40,32},{48,56},{56,48},{64,72... | collective-permute-start | bytes 393224 | tf_op jit(solution)/shard_map/ppermute | solution.py:488
  32.2 12.2 %collective-permute-start.12 = (bf16[2,128,512]{2,1,0:T(8,128)(2,1)S(1)}, bf16[2,128,512]{2,1,0:T(8,128)(2,1)S(1)}, u32[]{:S(2)}, u32[]{:S(2)}) collective-permute-start(bf16[2,128,512]{2,1,0:T(8,128)(2,1)S(1)} %collective-permute-done.11.two_ref), channel_id=1, source_target_pairs={{0,16},{8,120},{16,32},{24,8},{32,48},{40,24},{48,64},{56,40},{64,... | collective-permute-start | bytes 786440 | tf_op jit(solution)/shard_map/ppermute | solution.py:488
  35.6 8.8 %collective-permute-start.13 = (bf16[128,512]{1,0:T(8,128)(2,1)S(1)}, bf16[128,512]{1,0:T(8,128)(2,1)S(1)}, u32[]{:S(2)}, u32[]{:S(2)}) collective-permute-start(bf16[128,512]{1,0:T(8,128)(2,1)S(1)} %slice_bitcast_fusion), channel_id=1, source_target_pairs={{0,32},{8,104},{16,48},{24,120},{32,64},{40,8},{48,80},{56,24},{64... | collective-permute-start | bytes 393224 | tf_op jit(solution)/shard_map/ppermute | solution.py:488
  46.8 12.0 %copy-start = (bf16[256,4096]{1,0:T(8,128)(2,1)S(1)}, bf16[256,4096]{1,0:T(8,128)(2,1)}, u32[]{:S(2)}) copy-start(bf16[256,4096]{1,0:T(8,128)(2,1)} %w_ref.1) | copy-start | bytes 6291460
  46.8 1.5 %collective-permute-start.15 = (bf16[256,384]{1,0:T(8,128)(2,1)S(1)}, bf16[256,384]{1,0:T(8,128)(2,1)S(1)}, u32[]{:S(2)}, u32[]{:S(2)}) collective-permute-start(bf16[256,384]{1,0:T(8,128)(2,1)S(1)} %get-tuple-element.35), channel_id=1, source_target_pairs={{0,8},{8,0},{16,24},{24,16},{32,40},{40,32},{48,56},{56,48},{64,72... | collective-permute-start | bytes 589832 | tf_op jit(solution)/shard_map/ppermute | solution.py:488
  49.5 1.5 %collective-permute-start.16 = (bf16[256,384]{1,0:T(8,128)(2,1)S(1)}, bf16[256,384]{1,0:T(8,128)(2,1)S(1)}, u32[]{:S(2)}, u32[]{:S(2)}) collective-permute-start(bf16[256,384]{1,0:T(8,128)(2,1)S(1)} %get-tuple-element.39), channel_id=1, source_target_pairs={{0,8},{8,0},{16,24},{24,16},{32,40},{40,32},{48,56},{56,48},{64,72... | collective-permute-start | bytes 589832 | tf_op jit(solution)/shard_map/ppermute | solution.py:488
  49.7 9.1 %collective-permute-start.17 = (bf16[256,384]{1,0:T(8,128)(2,1)S(1)}, bf16[256,384]{1,0:T(8,128)(2,1)S(1)}, u32[]{:S(2)}, u32[]{:S(2)}) collective-permute-start(bf16[256,384]{1,0:T(8,128)(2,1)S(1)} %merge.2.refs_9_.upper_ref), channel_id=1, source_target_pairs={{0,128},{8,136},{16,144},{24,152},{32,160},{40,168},{48,176},{56,1... | collective-permute-start | bytes 589832 | tf_op jit(solution)/shard_map/ppermute | solution.py:488
  59.9 8.5 %collective-permute-start.18 = (bf16[32,4096]{1,0:T(8,128)(2,1)S(1)}, bf16[32,4096]{1,0:T(8,128)(2,1)S(1)}, u32[]{:S(2)}, u32[]{:S(2)}) collective-permute-start(bf16[32,4096]{1,0:T(8,128)(2,1)S(1)} %get-tuple-element.41), channel_id=1, source_target_pairs={{0,1},{1,2},{2,3},{3,0},{4,5},{5,6},{6,7},{7,4},{8,9},{9,10},{10,1... | collective-permute-start | bytes 786440 | tf_op jit(solution)/shard_map/ppermute | solution.py:496
  61.2 19.8 %collective-permute-start.19 = (bf16[32,4096]{1,0:T(8,128)(2,1)S(1)}, bf16[32,4096]{1,0:T(8,128)(2,1)S(1)}, u32[]{:S(2)}, u32[]{:S(2)}) collective-permute-start(bf16[32,4096]{1,0:T(8,128)(2,1)S(1)} %get-tuple-element.42), channel_id=1, source_target_pairs={{0,2},{1,3},{2,0},{3,1},{4,6},{5,7},{6,4},{7,5},{8,10},{9,11},{10,... | collective-permute-start | bytes 786440 | tf_op jit(solution)/shard_map/ppermute | solution.py:496
  62.8 18.2 %collective-permute-start.20 = (bf16[32,4096]{1,0:T(8,128)(2,1)S(1)}, bf16[32,4096]{1,0:T(8,128)(2,1)S(1)}, u32[]{:S(2)}, u32[]{:S(2)}) collective-permute-start(bf16[32,4096]{1,0:T(8,128)(2,1)S(1)} %get-tuple-element.43), channel_id=1, source_target_pairs={{0,3},{1,0},{2,1},{3,2},{4,7},{5,4},{6,5},{7,6},{8,11},{9,8},{10,9... | collective-permute-start | bytes 786440 | tf_op jit(solution)/shard_map/ppermute | solution.py:496
  65.3 15.7 %collective-permute-start.21 = (bf16[32,4096]{1,0:T(8,128)(2,1)S(1)}, bf16[32,4096]{1,0:T(8,128)(2,1)S(1)}, u32[]{:S(2)}, u32[]{:S(2)}) collective-permute-start(bf16[32,4096]{1,0:T(8,128)(2,1)S(1)} %get-tuple-element.44), channel_id=1, source_target_pairs={{0,4},{1,5},{2,6},{3,7},{4,0},{5,1},{6,2},{7,3},{8,12},{9,13},{10,... | collective-permute-start | bytes 786440 | tf_op jit(solution)/shard_map/ppermute | solution.py:496
  68.4 14.2 %collective-permute-start.22 = (bf16[32,4096]{1,0:T(8,128)(2,1)S(1)}, bf16[32,4096]{1,0:T(8,128)(2,1)S(1)}, u32[]{:S(2)}, u32[]{:S(2)}) collective-permute-start(bf16[32,4096]{1,0:T(8,128)(2,1)S(1)} %get-tuple-element.45), channel_id=1, source_target_pairs={{0,5},{1,6},{2,7},{3,4},{4,1},{5,2},{6,3},{7,0},{8,13},{9,14},{10,... | collective-permute-start | bytes 786440 | tf_op jit(solution)/shard_map/ppermute | solution.py:496
  68.4 27.1 %collective-permute-start.23 = (bf16[32,4096]{1,0:T(8,128)(2,1)S(1)}, bf16[32,4096]{1,0:T(8,128)(2,1)S(1)}, u32[]{:S(2)}, u32[]{:S(2)}) collective-permute-start(bf16[32,4096]{1,0:T(8,128)(2,1)S(1)} %get-tuple-element.46), channel_id=1, source_target_pairs={{0,6},{1,7},{2,4},{3,5},{4,2},{5,3},{6,0},{7,1},{8,14},{9,15},{10,... | collective-permute-start | bytes 786440 | tf_op jit(solution)/shard_map/ppermute | solution.py:496
  81.0 15.6 %collective-permute-start.24 = (bf16[32,4096]{1,0:T(8,128)(2,1)S(1)}, bf16[32,4096]{1,0:T(8,128)(2,1)S(1)}, u32[]{:S(2)}, u32[]{:S(2)}) collective-permute-start(bf16[32,4096]{1,0:T(8,128)(2,1)S(1)} %get-tuple-element.47), channel_id=1, source_target_pairs={{0,7},{1,4},{2,5},{3,6},{4,3},{5,0},{6,1},{7,2},{8,15},{9,12},{10,... | collective-permute-start | bytes 786440 | tf_op jit(solution)/shard_map/ppermute | solution.py:496
